TPU v7x, 32 devices: a whole 2x2x4 slice. The times are simulated.
32 devices in a mesh: dp: 8 (over y, x, core), fsdp: 4 (over z).
Axes of the slice: x: 2, y: 2, z: 4, core: 2. Of those that a mesh axis runs over, the one named last changes fastest.
Arguments:
- inputs: bfloat16 [8, 512, 1024], P('dp', 'fsdp'), may hold values from -6 to 6
- gain_mixer: bfloat16 [1024], P(('dp', 'fsdp')), may hold values from 0.5 to 1.5
- weight_in: bfloat16 [1024, 3072], P(('dp', 'fsdp')), may hold values from -0.1875 to 0.1875
- conv_taps: bfloat16 [3, 1024], P(None, ('dp', 'fsdp')), may hold values from -3.5 to 3.5
- weight_out: bfloat16 [1024, 1024], P(('dp', 'fsdp')), may hold values from -0.1875 to 0.1875
- gain_ffn: bfloat16 [1024], P(('dp', 'fsdp')), may hold values from 0.5 to 1.5
- weight_gate: bfloat16 [1024, 4608], P(('dp', 'fsdp')), may hold values from -0.1875 to 0.1875
- weight_up: bfloat16 [1024, 4608], P(('dp', 'fsdp')), may hold values from -0.1875 to 0.1875
- weight_down: bfloat16 [4608, 1024], P(('dp', 'fsdp')), may hold values from -0.09375 to 0.09375
- cotangent: bfloat16 [8, 512, 1024], P('dp', 'fsdp'), may hold values from -6 to 6
Outputs:
- outputs: bfloat16 [8, 512, 1024], P('dp', 'fsdp')
- grad_inputs: float32 [8, 512, 1024], P('dp', 'fsdp')
- grad_gain_mixer: float32 [1024], P(('dp', 'fsdp'))
- grad_weight_in: float32 [1024, 3072], P(('dp', 'fsdp'))
- grad_conv_taps: float32 [3, 1024], P(None, ('dp', 'fsdp'))
- grad_weight_out: float32 [1024, 1024], P(('dp', 'fsdp'))
- grad_gain_ffn: float32 [1024], P(('dp', 'fsdp'))
- grad_weight_gate: float32 [1024, 4608], P(('dp', 'fsdp'))
- grad_weight_up: float32 [1024, 4608], P(('dp', 'fsdp'))
- grad_weight_down: float32 [4608, 1024], P(('dp', 'fsdp'))
All inputs are finite; a program needn't handle non-finite values.
Results may differ from a plain program's by a relative error of at most 0.0088.
Values may be sent and summed in bfloat16 or wider, within the bound.
A program may use at most 192 MiB of HBM per device.

v0:
```python
import jax
import jax.numpy as jnp
from jax import lax
from jax.sharding import PartitionSpec as P

KW = 3


EPS = 1e-05


def product(left, right):
    return jnp.dot(left, right, preferred_element_type=jnp.float32)


def product_tn(left, right):
    return lax.dot_general(
        left, right, (((0,), (0,)), ((), ())), preferred_element_type=jnp.float32
    )


def product_nt(left, right):
    return lax.dot_general(
        left, right, (((1,), (1,)), ((), ())), preferred_element_type=jnp.float32
    )


def norm_forward(hidden, gain):
    scale = lax.rsqrt(jnp.mean(hidden * hidden, axis=-1, keepdims=True) + EPS)
    normed = hidden * scale
    return (normed, scale, normed * gain.astype(jnp.float32))


def norm_backward(dact, normed, scale, gain):
    dnormed = dact * gain.astype(jnp.float32)
    dhidden = scale * (dnormed - normed * jnp.mean(dnormed * normed, axis=-1, keepdims=True))
    return (dhidden, jnp.sum(dact * normed, axis=0))


def lagged(values, offset):
    zeros = jnp.zeros((offset, values.shape[1]), values.dtype)
    return jnp.concatenate([zeros, values[: values.shape[0] - offset]], axis=0)


def leading(values, offset):
    zeros = jnp.zeros((offset, values.shape[1]), values.dtype)
    return jnp.concatenate([values[offset:], zeros], axis=0)


def split_columns(block, lead, dp_count, fs_count):
    rows = block.shape[0]
    inner = block.shape[1] // (lead * dp_count * fs_count)
    pieces = block.reshape(rows, lead, dp_count, fs_count, inner).transpose(3, 0, 1, 2, 4)
    return pieces.reshape(fs_count, 1, rows, lead * dp_count * inner)


def join_rows(received, dp_count):
    fs_count = received.shape[1]
    rows = received.shape[2]
    columns = received.shape[3]
    inner = rows // dp_count
    pieces = received.reshape(fs_count, dp_count, inner, columns).transpose(1, 0, 2, 3)
    return pieces.reshape(fs_count * rows, columns)


def split_rows(block, dp_count, fs_count):
    total = block.shape[0]
    columns = block.shape[1]
    inner = total // (dp_count * fs_count)
    pieces = block.reshape(dp_count, fs_count, inner, columns).transpose(1, 0, 2, 3)
    return pieces.reshape(fs_count, 1, dp_count * inner, columns)


def join_columns(received, lead, dp_count):
    fs_count = received.shape[1]
    rows = received.shape[2]
    columns = received.shape[3]
    inner = columns // (lead * dp_count)
    pieces = received.reshape(fs_count, rows, lead, dp_count, inner).transpose(1, 2, 3, 0, 4)
    return pieces.reshape(rows, lead * dp_count * fs_count * inner)


def whole_sequence(rows):
    return lax.all_gather(rows, "fsdp", axis=0, tiled=True)


def token_share(partial_value):
    return lax.psum_scatter(partial_value, "fsdp", scatter_dimension=0, tiled=True)


def split_features(
    inputs,
    gain_mixer,
    weight_in,
    conv_taps,
    weight_out,
    gain_ffn,
    weight_gate,
    weight_up,
    weight_down,
    cotangent,
):
    dp_count = lax.axis_size("dp")
    fs_count = lax.axis_size("fsdp")
    gains = (
        lax.all_gather(gain_mixer, ("dp", "fsdp"), axis=0, tiled=True),
        lax.all_gather(gain_ffn, ("dp", "fsdp"), axis=0, tiled=True),
    )
    held_rows = (
        lax.all_gather(weight_in, "dp", axis=0, tiled=True),
        lax.all_gather(conv_taps, "dp", axis=1, tiled=True),
        lax.all_gather(weight_out, "dp", axis=0, tiled=True),
        lax.all_gather(weight_gate, "dp", axis=0, tiled=True),
        lax.all_gather(weight_up, "dp", axis=0, tiled=True),
        lax.all_gather(weight_down, "dp", axis=0, tiled=True),
    )
    in_rows, taps_part, out_rows, gate_rows, up_rows, down_rows = held_rows
    columns_moved = (
        lax.all_to_all(
            split_columns(in_rows, 3, dp_count, fs_count),
            "fsdp",
            split_axis=0,
            concat_axis=1,
            tiled=True,
        ),
        lax.all_to_all(
            split_columns(gate_rows, 1, dp_count, fs_count),
            "fsdp",
            split_axis=0,
            concat_axis=1,
            tiled=True,
        ),
        lax.all_to_all(
            split_columns(up_rows, 1, dp_count, fs_count),
            "fsdp",
            split_axis=0,
            concat_axis=1,
            tiled=True,
        ),
    )
    in_cols = join_rows(columns_moved[0], dp_count)
    gate_cols = join_rows(columns_moved[1], dp_count)
    up_cols = join_rows(columns_moved[2], dp_count)
    taps32 = taps_part.astype(jnp.float32)
    quarter = in_cols.shape[1] // 3
    hidden = inputs[0].astype(jnp.float32)
    grad_out = cotangent[0]
    normed1, scale1, pre1 = norm_forward(hidden, gains[0])
    act1 = pre1.astype(jnp.bfloat16)
    act1_all = whole_sequence(act1)
    projected = product(act1_all, in_cols)
    bpart = projected[:, :quarter]
    cpart = projected[:, quarter : 2 * quarter]
    xpart = projected[:, 2 * quarter :]
    gated = bpart * xpart
    lagged_rows = [lagged(gated, offset) for offset in range(KW)]
    conv = taps32[0] * lagged_rows[0]
    for offset in range(1, KW):
        conv = conv + taps32[offset] * lagged_rows[offset]
    act2 = (cpart * conv).astype(jnp.bfloat16)
    resid = hidden + token_share(product(act2, out_rows))
    normed2, scale2, pre2 = norm_forward(resid, gains[1])
    act3 = pre2.astype(jnp.bfloat16)
    act3_all = whole_sequence(act3)
    gate = product(act3_all, gate_cols)
    upval = product(act3_all, up_cols)
    sig = jax.nn.sigmoid(gate)
    act4 = (gate * sig * upval).astype(jnp.bfloat16)
    outputs = (resid + token_share(product(act4, down_rows))).astype(jnp.bfloat16)
    grad_all = whole_sequence(grad_out)
    g_down = product_tn(act4, grad_all)
    dact4 = product_nt(grad_all, down_rows)
    dgate = (dact4 * upval * sig * (1.0 + gate * (1.0 - sig))).astype(jnp.bfloat16)
    dupval = (dact4 * gate * sig).astype(jnp.bfloat16)
    g_gate = product_tn(act3_all, dgate)
    g_up = product_tn(act3_all, dupval)
    dact3 = token_share(product_nt(dgate, gate_cols) + product_nt(dupval, up_cols))
    dnorm2, g_gain2 = norm_backward(dact3, normed2, scale2, gains[1])
    dresid = grad_out.astype(jnp.float32) + dnorm2
    dres16 = dresid.astype(jnp.bfloat16)
    dres_all = whole_sequence(dres16)
    g_out = product_tn(act2, dres_all)
    dact2 = product_nt(dres_all, out_rows)
    dcpart = dact2 * conv
    dconv = dact2 * cpart
    g_taps = jnp.stack(
        [jnp.sum(dconv * lagged_rows[offset], axis=0) for offset in range(KW)], axis=0
    )
    dgated = taps32[0] * dconv
    for offset in range(1, KW):
        dgated = dgated + taps32[offset] * leading(dconv, offset)
    dproj = jnp.concatenate([dgated * xpart, dcpart, dgated * bpart], axis=1).astype(jnp.bfloat16)
    g_in = product_tn(act1_all, dproj)
    dact1 = token_share(product_nt(dproj, in_cols))
    dnorm1, g_gain1 = norm_backward(dact1, normed1, scale1, gains[0])
    grad_inputs = dresid + dnorm1
    rows_moved = (
        lax.all_to_all(
            split_rows(g_in, dp_count, fs_count).astype(jnp.bfloat16),
            "fsdp",
            split_axis=0,
            concat_axis=1,
            tiled=True,
        ).astype(jnp.float32),
        lax.all_to_all(
            split_rows(g_gate, dp_count, fs_count).astype(jnp.bfloat16),
            "fsdp",
            split_axis=0,
            concat_axis=1,
            tiled=True,
        ).astype(jnp.float32),
        lax.all_to_all(
            split_rows(g_up, dp_count, fs_count).astype(jnp.bfloat16),
            "fsdp",
            split_axis=0,
            concat_axis=1,
            tiled=True,
        ).astype(jnp.float32),
    )
    g_in_rows = join_columns(rows_moved[0], 3, dp_count)
    g_gate_rows = join_columns(rows_moved[1], 1, dp_count)
    g_up_rows = join_columns(rows_moved[2], 1, dp_count)
    owned = (
        lax.psum_scatter(g_in_rows, "dp", scatter_dimension=0, tiled=True),
        lax.psum_scatter(g_taps, "dp", scatter_dimension=1, tiled=True),
        lax.psum_scatter(g_out, "dp", scatter_dimension=0, tiled=True),
        lax.psum_scatter(g_gate_rows, "dp", scatter_dimension=0, tiled=True),
        lax.psum_scatter(g_up_rows, "dp", scatter_dimension=0, tiled=True),
        lax.psum_scatter(g_down, "dp", scatter_dimension=0, tiled=True),
    )
    gain_owned = (
        lax.psum_scatter(g_gain1, ("dp", "fsdp"), scatter_dimension=0, tiled=True),
        lax.psum_scatter(g_gain2, ("dp", "fsdp"), scatter_dimension=0, tiled=True),
    )
    return (
        outputs[None],
        grad_inputs[None],
        gain_owned[0],
        owned[0],
        owned[1],
        owned[2],
        gain_owned[1],
        owned[3],
        owned[4],
        owned[5],
    )


def on_device(
    inputs,
    gain_mixer,
    weight_in,
    conv_taps,
    weight_out,
    gain_ffn,
    weight_gate,
    weight_up,
    weight_down,
    cotangent,
):
    return split_features(
        inputs,
        gain_mixer,
        weight_in,
        conv_taps,
        weight_out,
        gain_ffn,
        weight_gate,
        weight_up,
        weight_down,
        cotangent,
    )


def solution(mesh):
    in_specs = (
        P("dp", "fsdp", None),
        P(("dp", "fsdp")),
        P(("dp", "fsdp"), None),
        P(None, ("dp", "fsdp")),
        P(("dp", "fsdp"), None),
        P(("dp", "fsdp")),
        P(("dp", "fsdp"), None),
        P(("dp", "fsdp"), None),
        P(("dp", "fsdp"), None),
        P("dp", "fsdp", None),
    )
    out_specs = (
        P("dp", "fsdp", None),
        P("dp", "fsdp", None),
        P(("dp", "fsdp")),
        P(("dp", "fsdp"), None),
        P(None, ("dp", "fsdp")),
        P(("dp", "fsdp"), None),
        P(("dp", "fsdp")),
        P(("dp", "fsdp"), None),
        P(("dp", "fsdp"), None),
        P(("dp", "fsdp"), None),
    )
    return jax.shard_map(
        on_device, mesh=mesh, in_specs=in_specs, out_specs=out_specs, check_vma=False
    )
```

profile of v0, /device:TPU:0, one launch (start us, length us, event | category | flops | bytes accessed | tf_op | source)
XLA Modules:
  0.0 928.9 jit_solution(4280727826086993456)
XLA Ops:
  9.7 41.9 %all-reduce.9 = (bf16[1024]{0:T(1024)(128)(2,1)S(1)}, bf16[1024]{0:T(1024)(128)(2,1)S(1)}) all-reduce(bf16[1024]{0:T(1024)(128)(2,1)S(1)} %dynamic-update-slice, bf16[1024]{0:T(1024)(128)(2,1)S(1)} %dynamic-update-slice.1), channel_id=1, replica_groups=mesh['dp'=8,'fsdp'=4] {'dp','fsdp'}, use_global_device_ids=true, to_apply=%add.4 | all-reduce | flops 2048 | bytes 8192
  62.2 9.7 %all-gather.1 = bf16[8,32,3]{1,2,0:T(4,128)(2,1)S(1)} all-gather(bf16[1,32,3]{1,2,0:T(4,128)(2,1)S(1)} %bitcast.177), channel_id=1, replica_groups=mesh['dp'=8,'fsdp'=4] {'dp'}, dimensions={0}, use_global_device_ids=true | all-gather | bytes 1728 | tf_op jit(solution)/shard_map/all_gather | solution.py:111
  71.9 8.9 all_gather.40
  80.8 34.4 %all-to-all-done = bf16[4,1,256,768]{2,3,1,0:T(8,128)(2,1)S(1)} async-done(((bf16[4,1,256,768]{2,3,1,0:T(8,128)(2,1)}), bf16[4,1,256,768]{2,3,1,0:T(8,128)(2,1)S(1)}, u32[]{:S(2)}, u32[]{:S(2)}) %all-to-all-start) | async-done | bytes 1572896 | tf_op jit(solution)/shard_map/all_to_all | solution.py:119
  125.9 12.1 %all-gather.17.cloned.1.call-done = bf16[256,4608]{1,0:T(8,128)(2,1)} async-done(((bf16[32,4608]{1,0:T(8,128)(2,1)}), bf16[256,4608]{1,0:T(8,128)(2,1)}) %all-gather.17.cloned.1.call-update) | async-done | bytes 2359312 | tf_op jit(solution)/shard_map/all_gather | solution.py:113
  138.0 4.3 copy.104
  145.6 4.7 all-to-all-start.1
  150.3 60.8 %reduce-scatter.19.cloned.1.call-done = f32[128,1024]{1,0:T(8,128)} async-done(((f32[512,1024]{1,0:T(8,128)}), f32[128,1024]{1,0:T(8,128)}) %reduce-scatter.19.cloned.1.call-update) | async-done | bytes 524304 | tf_op jit(solution)/shard_map/reduce_scatter | solution.py:88
  213.9 43.3 %all-gather.19.cloned.1.call-done = bf16[256,4608]{1,0:T(8,128)(2,1)} async-done(((bf16[32,4608]{1,0:T(8,128)(2,1)}), bf16[256,4608]{1,0:T(8,128)(2,1)}) %all-gather.19.cloned.1.call-update) | async-done | bytes 2359312 | tf_op jit(solution)/shard_map/all_gather | solution.py:114
  257.2 4.3 copy.109
  264.8 4.6 all-to-all-start.2
  270.3 4.3 copy.107
  278.0 76.8 %all-to-all-done.2 = bf16[4,1,256,1152]{2,3,1,0:T(8,128)(2,1)} async-done(((bf16[4,1,256,1152]{2,3,1,0:T(8,128)(2,1)}), bf16[4,1,256,1152]{2,3,1,0:T(8,128)(2,1)}, u32[]{:S(2)}, u32[]{:S(2)}) %all-to-all-start.2) | async-done | bytes 2359328 | tf_op jit(solution)/shard_map/all_to_all | solution.py:133
  354.8 4.3 copy.112
  362.6 5.1 fusion.24
  370.7 10.0 %all-gather.21.cloned.1.call-done = bf16[1152,1024]{1,0:T(8,128)(2,1)} async-done(((bf16[144,1024]{1,0:T(8,128)(2,1)}), bf16[1152,1024]{1,0:T(8,128)(2,1)}) %all-gather.21.cloned.1.call-update) | async-done | bytes 2359312 | tf_op jit(solution)/shard_map/all_gather | solution.py:115
  380.7 6.8 multiply_convert_fusion
  393.0 43.7 %reduce-scatter.23.cloned.1.call-done = f32[128,1024]{1,0:T(8,128)} async-done(((f32[512,1024]{1,0:T(8,128)}), f32[128,1024]{1,0:T(8,128)}) %reduce-scatter.23.cloned.1.call-update) | async-done | bytes 524304 | tf_op jit(solution)/shard_map/reduce_scatter | solution.py:88
  440.0 27.3 %all-gather.23.cloned.1.call-done = bf16[512,1024]{1,0:T(8,128)(2,1)} async-done(((bf16[128,1024]{1,0:T(8,128)(2,1)}), bf16[512,1024]{1,0:T(8,128)(2,1)}) %all-gather.23.cloned.1.call-update) | async-done | bytes 1048592 | tf_op jit(solution)/shard_map/all_gather | solution.py:84
  472.7 4.1 fusion.16
  476.9 4.5 fusion.26
  481.7 4.8 fusion
  492.3 4.6 all-to-all-start.4
  498.6 85.7 %all-to-all-done.4 = bf16[4,1,256,1152]{3,2,1,0:T(8,128)(2,1)} async-done(((bf16[4,1,256,1152]{3,2,1,0:T(8,128)(2,1)}), bf16[4,1,256,1152]{3,2,1,0:T(8,128)(2,1)}, u32[]{:S(2)}, u32[]{:S(2)}) %all-to-all-start.4) | async-done | bytes 2359328 | tf_op jit(solution)/shard_map/all_to_all | solution.py:205
  590.4 6.2 copy.133
  600.0 79.0 %all_to_all.24 = bf16[4,1,256,1152]{3,2,1,0:T(8,128)(2,1)} all-to-all(bf16[4,1,256,1152]{3,2,1,0:T(8,128)(2,1)S(1)} %bitcast.150), channel_id=1, replica_groups=mesh['dp'=8,'fsdp'=4] {'fsdp'}, dimensions={0} | all-to-all | bytes 4718592 | tf_op jit(solution)/shard_map/all_to_all | solution.py:212
  685.0 6.6 copy.135
  694.3 39.1 %all_to_all.25 = bf16[4,1,256,768]{3,2,1,0:T(8,128)(2,1)S(1)} all-to-all(bf16[4,1,256,768]{3,2,1,0:T(8,128)(2,1)S(1)} %bitcast.154), channel_id=1, replica_groups=mesh['dp'=8,'fsdp'=4] {'fsdp'}, dimensions={0} | all-to-all | bytes 3145728 | tf_op jit(solution)/shard_map/all_to_all | solution.py:198
  745.1 39.1 %all-reduce.8 = (f32[1024]{0:T(1024)S(1)}, f32[1024]{0:T(1024)S(1)}) all-reduce(f32[1024]{0:T(1024)S(1)} %get-tuple-element.52, f32[1024]{0:T(1024)S(1)} %get-tuple-element.50), channel_id=7, replica_groups=mesh['dp'=8,'fsdp'=4] {'dp','fsdp'}, use_global_device_ids=true, to_apply=%region_9.0.clone | all-reduce | flops 2048 | bytes 16384
  787.7 26.8 %reduce-scatter.35.cloned.1.call-done = f32[32,4608]{1,0:T(8,128)} async-done(((f32[256,4608]{1,0:T(8,128)}), f32[32,4608]{1,0:T(8,128)}) %reduce-scatter.35.cloned.1.call-update) | async-done | bytes 589840
  814.5 57.7 %reduce-scatter.37.cloned.1.call-done = f32[32,4608]{1,0:T(8,128)} async-done(((f32[256,4608]{1,0:T(8,128)}), f32[32,4608]{1,0:T(8,128)}) %reduce-scatter.37.cloned.1.call-update) | async-done | bytes 589840
  872.2 49.9 %reduce-scatter.31.cloned.1.call-done = f32[32,3072]{1,0:T(8,128)} async-done(((f32[256,3072]{1,0:T(8,128)}), f32[32,3072]{1,0:T(8,128)}) %reduce-scatter.31.cloned.1.call-update) | async-done | bytes 393232
  (152 shorter events, 98.7 us)
Async XLA Ops:
  7.2 48.1 %all-gather.13.cloned.1.call-start = ((), (), s32[]{:S(2)}) async-start(), calls=%async_computation.17 | async-start | bytes 1769472 | tf_op jit(solution)/shard_map/all_gather | solution.py:110
  7.9 111.7 %all-gather.11.cloned.1.call-start = ((), (), s32[]{:S(2)}) async-start(), calls=%async_computation.16 | async-start | bytes 1310720 | tf_op jit(solution)/shard_map/all_gather | solution.py:84
  54.5 83.5 %all-gather.17.cloned.1.call-start = ((), (), s32[]{:S(2)}) async-start(), calls=%async_computation.20 | async-start | bytes 2654208 | tf_op jit(solution)/shard_map/all_gather | solution.py:113
  58.3 13.6 %copy-start.12 = (bf16[32,1024]{1,0:T(8,128)(2,1)S(1)}, bf16[32,1024]{1,0:T(8,128)(2,1)}, u32[]{:S(2)}) copy-start(bf16[32,1024]{1,0:T(8,128)(2,1)} %param.14) | copy-start | bytes 196612
  58.3 56.9 %all-to-all-start = ((bf16[4,1,256,768]{2,3,1,0:T(8,128)(2,1)}), bf16[4,1,256,768]{2,3,1,0:T(8,128)(2,1)S(1)}, u32[]{:S(2)}, u32[]{:S(2)}) async-start(bf16[4,1,256,768]{2,3,1,0:T(8,128)(2,1)} %bitcast.151), calls=%async_computation | async-start | bytes 3145728 | tf_op jit(solution)/shard_map/all_to_all | solution.py:119
  62.2 148.9 %reduce-scatter.19.cloned.1.call-start = ((), (), s32[]{:S(2)}) async-start(), calls=%async_computation.18 | async-start | bytes 2621440 | tf_op jit(solution)/shard_map/reduce_scatter | solution.py:88
  80.8 42.6 %copy-start.1 = (bf16[256,1024]{1,0:T(8,128)(2,1)}, bf16[256,1024]{1,0:T(8,128)(2,1)S(1)}, u32[]{:S(2)}) copy-start(bf16[256,1024]{1,0:T(8,128)(2,1)S(1)} %all_gather.40) | copy-start | bytes 1572868
  125.3 131.9 %all-gather.19.cloned.1.call-start = ((), (), s32[]{:S(2)}) async-start(), calls=%async_computation.21 | async-start | bytes 2654208 | tf_op jit(solution)/shard_map/all_gather | solution.py:114
  145.6 65.5 %copy-start = (bf16[1,128,1024]{2,1,0:T(8,128)(2,1)S(1)}, bf16[1,128,1024]{2,1,0:T(8,128)(2,1)}, u32[]{:S(2)}) copy-start(bf16[1,128,1024]{2,1,0:T(8,128)(2,1)} %param.10) | copy-start | bytes 786436
  145.6 119.2 %all-to-all-start.1 = ((bf16[4,1,256,1152]{2,3,1,0:T(8,128)(2,1)}), bf16[4,1,256,1152]{2,3,1,0:T(8,128)(2,1)}, u32[]{:S(2)}, u32[]{:S(2)}) async-start(bf16[4,1,256,1152]{2,3,1,0:T(8,128)(2,1)} %bitcast.144), calls=%async_computation.2 | async-start | bytes 4718592 | tf_op jit(solution)/shard_map/all_to_all | solution.py:126
  150.3 212.3 %all-gather.15.cloned.1.call-start = ((), (), s32[]{:S(2)}) async-start(), calls=%async_computation.19 | async-start | bytes 1310720 | tf_op jit(solution)/shard_map/all_gather | solution.py:84
  213.1 157.5 %all-gather.25.cloned.1.call-start = ((), (), s32[]{:S(2)}) async-start(), calls=%async_computation.29 | async-start | bytes 1310720 | tf_op jit(solution)/shard_map/all_gather | solution.py:84
  264.8 90.1 %all-to-all-start.2 = ((bf16[4,1,256,1152]{2,3,1,0:T(8,128)(2,1)}), bf16[4,1,256,1152]{2,3,1,0:T(8,128)(2,1)}, u32[]{:S(2)}, u32[]{:S(2)}) async-start(bf16[4,1,256,1152]{2,3,1,0:T(8,128)(2,1)} %bitcast.145), calls=%async_computation.3 | async-start | bytes 4718592 | tf_op jit(solution)/shard_map/all_to_all | solution.py:133
  269.4 111.3 %all-gather.21.cloned.1.call-start = ((), (), s32[]{:S(2)}) async-start(), calls=%async_computation.22 | async-start | bytes 2654208 | tf_op jit(solution)/shard_map/all_gather | solution.py:115
  270.1 166.6 %reduce-scatter.23.cloned.1.call-start = ((), (), s32[]{:S(2)}) async-start(), calls=%async_computation.24 | async-start | bytes 2621440 | tf_op jit(solution)/shard_map/reduce_scatter | solution.py:88
  362.6 5.1 copy-start.5
  362.6 5.1 copy-start.15
  380.7 6.8 copy-start.4
  392.9 45.1 %copy-start.7 = (bf16[1,128,1024]{2,1,0:T(8,128)(2,1)S(1)}, bf16[1,128,1024]{2,1,0:T(8,128)(2,1)}, u32[]{:S(2)}) copy-start(bf16[1,128,1024]{2,1,0:T(8,128)(2,1)} %param.19) | copy-start | bytes 786436
  392.9 74.4 %all-gather.23.cloned.1.call-start = ((), (), s32[]{:S(2)}) async-start(), calls=%async_computation.25 | async-start | bytes 1310720 | tf_op jit(solution)/shard_map/all_gather | solution.py:84
  440.0 302.4 %reduce-scatter.33.cloned.1.call-start = ((), (), s32[]{:S(2)}) async-start(), calls=%async_computation.31 | async-start | bytes 147456
  472.7 271.1 %reduce-scatter.25.cloned.1.call-start = ((), (), s32[]{:S(2)}) async-start(), calls=%async_computation.26 | async-start | bytes 2621440 | tf_op jit(solution)/shard_map/reduce_scatter | solution.py:88
  472.7 4.2 copy-start.8
  476.8 308.5 %reduce-scatter.21.cloned.1.call-start = ((), (), s32[]{:S(2)}) async-start(), calls=%async_computation.23 | async-start | bytes 2621440 | tf_op jit(solution)/shard_map/reduce_scatter | solution.py:88
  481.4 306.2 %reduce-scatter.29.cloned.1.call-start = ((), (), s32[]{:S(2)}) async-start(), calls=%async_computation.28 | async-start | bytes 5308416 | tf_op jit(solution)/shard_map/reduce_scatter | solution.py:229
  492.3 4.7 copy-start.3
  492.3 92.0 %all-to-all-start.4 = ((bf16[4,1,256,1152]{3,2,1,0:T(8,128)(2,1)}), bf16[4,1,256,1152]{3,2,1,0:T(8,128)(2,1)}, u32[]{:S(2)}, u32[]{:S(2)}) async-start(bf16[4,1,256,1152]{3,2,1,0:T(8,128)(2,1)} %bitcast.46), calls=%async_computation.9 | async-start | bytes 4718592 | tf_op jit(solution)/shard_map/all_to_all | solution.py:205
  496.9 290.7 %reduce-scatter.27.cloned.1.call-start = ((), (), s32[]{:S(2)}) async-start(), calls=%async_computation.27 | async-start | bytes 1179648 | tf_op jit(solution)/shard_map/reduce_scatter | solution.py:226
  498.6 315.9 %reduce-scatter.35.cloned.1.call-start = ((), (), s32[]{:S(2)}) async-start(), calls=%async_computation.32 | async-start | bytes 5308416
  596.6 275.5 %reduce-scatter.37.cloned.1.call-start = ((), (), s32[]{:S(2)}) async-start(), calls=%async_computation.33 | async-start | bytes 5308416
  691.7 230.4 %reduce-scatter.31.cloned.1.call-start = ((), (), s32[]{:S(2)}) async-start(), calls=%async_computation.30 | async-start | bytes 3538944
  742.3 43.0 %copy-start.2 = (f32[128,1024]{1,0:T(8,128)S(1)}, f32[128,1024]{1,0:T(8,128)}, u32[]{:S(2)}) copy-start(f32[128,1024]{1,0:T(8,128)} %reduce-scatter.23.cloned.1.call-done) | copy-start | bytes 1572868
  (11 other events, 18.1 us)
Sparse Core Ops, SparseCore 0:
  9.9 28.3 all-gather.12
  54.6 53.4 all-gather.10
  110.1 27.9 all-gather.16
  140.2 70.8 reduce-scatter.18
  212.8 44.3 all-gather.18
  259.2 48.0 all-gather.14
  308.8 42.8 all-gather.24
  353.6 27.0 all-gather.20
  393.1 43.6 reduce-scatter.22
  440.1 27.1 all-gather.22
  472.8 32.9 reduce-scatter.32
  507.9 73.8 reduce-scatter.24
  584.1 66.6 reduce-scatter.20
  654.6 62.4 reduce-scatter.28
  720.8 35.9 reduce-scatter.26
  760.6 53.7 reduce-scatter.34
  818.3 53.7 reduce-scatter.36
  876.0 46.0 reduce-scatter.30
where the time goes:
time: 931 us; the launch traced here: 929 us
  waiting for transfers between devices  532 us (57%)
  blocking collectives  218 us (23%)
  local copies, waits for them, and re-layouts  81.2 us (9%)
  matrix products  47 us (5%)
  starting transfers between devices  18.8 us (2%)
  other arithmetic  17.4 us (2%)
  between operations  14.6 us (2%)
    unnamed x22, waiting for transfers between devices  138 us
    reduce_scatter x4, waiting for transfers between devices, token_share(): lax.psum_scatter(partial_value, 'fsdp', scatter_dimension=0, tiled=True)  105 us
    all_to_all x1, waiting for transfers between devices, split_features(): lax.all_to_all(split_rows(g_gate, dp_count, fs_count).astype(jnp.bfloat16...  85.7 us
    unnamed x2, blocking collectives  81 us
    all_to_all x1, blocking collectives, split_features(): lax.all_to_all(split_rows(g_up, dp_count, fs_count).astype(jnp.bfloat16),...  79 us
    all_to_all x1, waiting for transfers between devices, split_features(): lax.all_to_all(split_columns(up_rows, 1, dp_count, fs_count), 'fsdp', spl...  76.8 us
    all_gather x1, waiting for transfers between devices, split_features(): lax.all_gather(weight_up, 'dp', axis=0, tiled=True)  43.3 us
    all_to_all x1, blocking collectives, split_features(): lax.all_to_all(split_rows(g_in, dp_count, fs_count).astype(jnp.bfloat16),...  39.1 us
  transfers between devices with their start and end apart: 22, of which 12 were waited for; matrix products, arithmetic and copies ran while one was open for 13% of the time, Pallas kernels for 0%

commit v1 on v0

v1 whole, which is shorter than its diff:
```python
import jax
import jax.numpy as jnp
from jax import lax
from jax.sharding import PartitionSpec as P

KW = 3


EPS = 1e-05

GRAD = jnp.float32


def product(left, right):
    return jnp.dot(left, right, preferred_element_type=jnp.float32)


def product_tn(left, right):
    return lax.dot_general(
        left, right, (((0,), (0,)), ((), ())), preferred_element_type=jnp.float32
    )


def product_nt(left, right):
    return lax.dot_general(
        left, right, (((1,), (1,)), ((), ())), preferred_element_type=jnp.float32
    )


def norm_forward(hidden, gain):
    scale = lax.rsqrt(jnp.mean(hidden * hidden, axis=-1, keepdims=True) + EPS)
    normed = hidden * scale
    return (normed, scale, normed * gain.astype(jnp.float32))


def norm_backward(dact, normed, scale, gain):
    dnormed = dact * gain.astype(jnp.float32)
    dhidden = scale * (dnormed - normed * jnp.mean(dnormed * normed, axis=-1, keepdims=True))
    return (dhidden, jnp.sum(dact * normed, axis=0))


def lagged(values, offset):
    zeros = jnp.zeros((offset, values.shape[1]), values.dtype)
    return jnp.concatenate([zeros, values[: values.shape[0] - offset]], axis=0)


def leading(values, offset):
    zeros = jnp.zeros((offset, values.shape[1]), values.dtype)
    return jnp.concatenate([values[offset:], zeros], axis=0)


def whole_sequence(rows):
    return lax.all_gather(rows, "fsdp", axis=0, tiled=True)


def token_share(partial_value):
    fs_count = lax.axis_size("fsdp")
    rows, columns = partial_value.shape
    pieces = partial_value.astype(jnp.bfloat16).reshape(fs_count, rows // fs_count, columns)
    received = lax.all_to_all(pieces, "fsdp", split_axis=0, concat_axis=0, tiled=True)
    return jnp.sum(received.astype(jnp.float32), axis=0)


def column_blocks(shard, lead, dp_count, fs_count):
    rows, columns = shard.shape
    inner = columns // (lead * dp_count * fs_count)
    pieces = shard.reshape(rows, lead, dp_count, fs_count, inner).transpose(3, 0, 1, 2, 4)
    return pieces.reshape(fs_count, rows, lead * dp_count * inner)


def column_join(blocks, lead, dp_count, fs_count):
    _, rows, columns = blocks.shape
    inner = columns // (lead * dp_count)
    pieces = blocks.reshape(fs_count, rows, lead, dp_count, inner).transpose(1, 2, 3, 0, 4)
    return pieces.reshape(rows, lead * dp_count * fs_count * inner)


def exchange(blocks):
    return lax.all_to_all(blocks, "fsdp", split_axis=0, concat_axis=0, tiled=True)


def gather_dp(rows):
    return lax.all_gather(rows, "dp", axis=0, tiled=True)


def reduce_dp(partial_grad):
    return lax.psum_scatter(partial_grad, "dp", scatter_dimension=0, tiled=True)


def split_features(
    inputs,
    gain_mixer,
    weight_in,
    conv_taps,
    weight_out,
    gain_ffn,
    weight_gate,
    weight_up,
    weight_down,
    cotangent,
):
    dp_count = lax.axis_size("dp")
    fs_count = lax.axis_size("fsdp")
    width = weight_out.shape[1]
    part = weight_out.shape[0]
    quarter = dp_count * part
    hid = dp_count * weight_down.shape[0]

    x_all = whole_sequence(inputs[0])
    small = jnp.concatenate([gain_mixer[None], gain_ffn[None], conv_taps], axis=0)
    small_all = lax.all_gather(small, ("dp", "fsdp"), axis=1, tiled=True)
    gain1, gain2 = small_all[0], small_all[1]
    taps32 = lax.dynamic_index_in_dim(
        small_all[2:].reshape(KW, dp_count, fs_count, part),
        lax.axis_index("fsdp"),
        axis=2,
        keepdims=False,
    ).reshape(KW, quarter).astype(jnp.float32)

    in_blocks = exchange(column_blocks(weight_in, 3, dp_count, fs_count))
    gu_blocks = exchange(
        jnp.concatenate(
            [
                column_blocks(weight_gate, 1, dp_count, fs_count),
                column_blocks(weight_up, 1, dp_count, fs_count),
            ],
            axis=2,
        )
    )
    in_cols = gather_dp(in_blocks.reshape(fs_count * part, 3 * quarter))
    out_rows = gather_dp(weight_out)
    gu_cols = gather_dp(gu_blocks.reshape(fs_count * part, 2 * hid))
    down_rows = gather_dp(weight_down)
    grad_out = cotangent[0]
    grad_all = whole_sequence(grad_out)

    _, _, pre1_all = norm_forward(x_all.astype(jnp.float32), gain1)
    act1_all = pre1_all.astype(jnp.bfloat16)
    projected = product(act1_all, in_cols)
    bpart = projected[:, :quarter]
    cpart = projected[:, quarter : 2 * quarter]
    xpart = projected[:, 2 * quarter :]
    gated = bpart * xpart
    lagged_rows = [lagged(gated, offset) for offset in range(KW)]
    conv = taps32[0] * lagged_rows[0]
    for offset in range(1, KW):
        conv = conv + taps32[offset] * lagged_rows[offset]
    act2 = (cpart * conv).astype(jnp.bfloat16)
    hidden = inputs[0].astype(jnp.float32)
    normed1, scale1, _ = norm_forward(hidden, gain1)
    resid = hidden + token_share(product(act2, out_rows))
    normed2, scale2, pre2 = norm_forward(resid, gain2)
    act3_all = whole_sequence(pre2.astype(jnp.bfloat16))
    gate_up = product(act3_all, gu_cols)
    gate, upval = gate_up[:, :hid], gate_up[:, hid:]
    sig = jax.nn.sigmoid(gate)
    act4 = (gate * sig * upval).astype(jnp.bfloat16)
    dact4 = product_nt(grad_all, down_rows)
    dgate = (dact4 * upval * sig * (1.0 + gate * (1.0 - sig))).astype(jnp.bfloat16)
    dupval = (dact4 * gate * sig).astype(jnp.bfloat16)
    dgu = jnp.concatenate([dgate, dupval], axis=1)
    dact3 = token_share(product_nt(dgu, gu_cols))
    outputs = (resid + token_share(product(act4, down_rows))).astype(jnp.bfloat16)
    g_gu = reduce_dp(product_tn(act3_all, dgu).astype(GRAD))
    g_down = reduce_dp(product_tn(act4, grad_all).astype(GRAD))
    dnorm2, g_gain2 = norm_backward(dact3, normed2, scale2, gain2)
    dresid = grad_out.astype(jnp.float32) + dnorm2
    dres_all = whole_sequence(dresid.astype(jnp.bfloat16))
    dact2 = product_nt(dres_all, out_rows)
    dcpart = dact2 * conv
    dconv = dact2 * cpart
    g_taps = jnp.stack(
        [jnp.sum(dconv * lagged_rows[offset], axis=0) for offset in range(KW)], axis=0
    )
    dgated = taps32[0] * dconv
    for offset in range(1, KW):
        dgated = dgated + taps32[offset] * leading(dconv, offset)
    dproj = jnp.concatenate([dgated * xpart, dcpart, dgated * bpart], axis=1).astype(jnp.bfloat16)
    dact1 = token_share(product_nt(dproj, in_cols))
    g_in = reduce_dp(product_tn(act1_all, dproj).astype(GRAD))
    g_out = reduce_dp(product_tn(act2, dres_all).astype(GRAD))
    dnorm1, g_gain1 = norm_backward(dact1, normed1, scale1, gain1)
    grad_inputs = dresid + dnorm1

    g_gu_owned = exchange(g_gu.reshape(fs_count, part, 2 * hid).astype(jnp.bfloat16)).astype(jnp.float32)
    g_in_owned = exchange(g_in.reshape(fs_count, part, 3 * quarter).astype(jnp.bfloat16)).astype(jnp.float32)
    own_column = (jnp.arange(fs_count) == lax.axis_index("fsdp"))[None, None, :, None]
    taps_spread = jnp.where(own_column, g_taps.reshape(KW, dp_count, 1, part), 0.0).reshape(KW, width)
    small_owned = lax.psum_scatter(
        jnp.concatenate([g_gain1[None], g_gain2[None], taps_spread], axis=0),
        ("dp", "fsdp"),
        scatter_dimension=1,
        tiled=True,
    )
    return (
        outputs[None],
        grad_inputs[None],
        small_owned[0],
        column_join(g_in_owned, 3, dp_count, fs_count),
        small_owned[2:],
        g_out.astype(jnp.float32),
        small_owned[1],
        column_join(g_gu_owned[:, :, :hid], 1, dp_count, fs_count),
        column_join(g_gu_owned[:, :, hid:], 1, dp_count, fs_count),
        g_down.astype(jnp.float32),
    )


def on_device(
    inputs,
    gain_mixer,
    weight_in,
    conv_taps,
    weight_out,
    gain_ffn,
    weight_gate,
    weight_up,
    weight_down,
    cotangent,
):
    return split_features(
        inputs,
        gain_mixer,
        weight_in,
        conv_taps,
        weight_out,
        gain_ffn,
        weight_gate,
        weight_up,
        weight_down,
        cotangent,
    )


def solution(mesh):
    in_specs = (
        P("dp", "fsdp", None),
        P(("dp", "fsdp")),
        P(("dp", "fsdp"), None),
        P(None, ("dp", "fsdp")),
        P(("dp", "fsdp"), None),
        P(("dp", "fsdp")),
        P(("dp", "fsdp"), None),
        P(("dp", "fsdp"), None),
        P(("dp", "fsdp"), None),
        P("dp", "fsdp", None),
    )
    out_specs = (
        P("dp", "fsdp", None),
        P("dp", "fsdp", None),
        P(("dp", "fsdp")),
        P(("dp", "fsdp"), None),
        P(None, ("dp", "fsdp")),
        P(("dp", "fsdp"), None),
        P(("dp", "fsdp")),
        P(("dp", "fsdp"), None),
        P(("dp", "fsdp"), None),
        P(("dp", "fsdp"), None),
    )
    return jax.shard_map(
        on_device, mesh=mesh, in_specs=in_specs, out_specs=out_specs, check_vma=False
    )
```

time: 931 us -> 716 us (0.77)
  waiting for transfers between devices: 532 us -> 411 us
  local copies, waits for them, and re-layouts: 81.2 us -> 32.7 us
  blocking collectives: 218 us -> 179 us
    all_to_all x4, waiting for transfers between devices: 197 us -> 47.7 us  [the longest x2 47.7 us: token_share(): lax.all_to_all(pieces, 'fsdp', split_axis=0, concat_axis=0, tiled=True)]
    unnamed x2 -> x0, blocking collectives: 81 us -> none
    all_gather x2, blocking collectives: 18.6 us -> 75.7 us  [the longest x1 67 us: split_features(): small_all = lax.all_gather(small, ('dp', 'fsdp'), axis=1, tiled=True)]
    all_gather x4, waiting for transfers between devices: 27.3 us -> 48.3 us  [whole_sequence(): return lax.all_gather(rows, 'fsdp', axis=0, tiled=True)]
    unnamed x53 -> x49, local copies, waits for them, and re-layouts: 26.5 us -> 8.25 us
    transpose x6 -> x0, local copies, waits for them, and re-layouts: 17.6 us -> none  [the longest x3 9.66 us: join_rows(): received.reshape(fs_count, dp_count, inner, columns).transpose(1, 0, 2, 3)]
    all_to_all x6 -> x0, local copies, waits for them, and re-layouts: 17.4 us -> none  [the longest x1 4.33 us: split_features(): lax.all_to_all(split_columns(gate_rows, 1, dp_count, fs_count), 'fsdp', s...]
    all_to_all x2 -> x4, blocking collectives: 118 us -> 103 us  [the longest x2 59.7 us: token_share(): lax.all_to_all(pieces, 'fsdp', split_axis=0, concat_axis=0, tiled=True)]
  transfers between devices with their start and end apart: 22 -> 16, of which waited for: 12 -> 10; matrix products, arithmetic and copies ran while one was open for 13% -> 9% of each run, Pallas kernels for 0% -> 0%
where the time goes in v1:
time: 716 us; the launch traced here: 715 us
  waiting for transfers between devices  411 us (57%)
  blocking collectives  179 us (25%)
  matrix products  46.8 us (7%)
  local copies, waits for them, and re-layouts  32.7 us (5%)
  starting transfers between devices  16.6 us (2%)
  between operations  14.7 us (2%)
  other arithmetic  13.8 us (2%)
    unnamed x13, waiting for transfers between devices  133 us
    reduce_scatter x4, waiting for transfers between devices, reduce_dp(): return lax.psum_scatter(partial_grad, 'dp', scatter_dimension=0, tiled=True)  115 us
    all_gather x3, waiting for transfers between devices, gather_dp(): return lax.all_gather(rows, 'dp', axis=0, tiled=True)  67.3 us
    all_gather x1, blocking collectives, split_features(): small_all = lax.all_gather(small, ('dp', 'fsdp'), axis=1, tiled=True)  67 us
    all_to_all x2, blocking collectives, token_share(): lax.all_to_all(pieces, 'fsdp', split_axis=0, concat_axis=0, tiled=True)  59.7 us
    all_gather x4, waiting for transfers between devices, whole_sequence(): return lax.all_gather(rows, 'fsdp', axis=0, tiled=True)  48.3 us
    all_to_all x2, waiting for transfers between devices, token_share(): lax.all_to_all(pieces, 'fsdp', split_axis=0, concat_axis=0, tiled=True)  47.7 us
    all_to_all x2, blocking collectives, exchange(): lax.all_to_all(blocks, 'fsdp', split_axis=0, concat_axis=0, tiled=True)  43.1 us
  transfers between devices with their start and end apart: 16, of which 10 were waited for; matrix products, arithmetic and copies ran while one was open for 9% of the time, Pallas kernels for 0%

profile of v1, /device:TPU:0, one launch (start us, length us, event | category | flops | bytes accessed | tf_op | source)
XLA Modules:
  0.0 714.6 jit_solution(8151902977022275739)
XLA Ops:
  10.1 13.9 %all_to_all.40 = bf16[4,32,768]{2,1,0:T(8,128)(2,1)} all-to-all(bf16[4,32,768]{2,1,0:T(8,128)(2,1)S(1)} %reshape.248), channel_id=1, replica_groups=mesh['dp'=8,'fsdp'=4] {'fsdp'}, dimensions={0} | all-to-all | bytes 393216 | tf_op jit(solution)/shard_map/all_to_all | solution.py:79
  24.1 67.0 %all-gather.2 = bf16[32,32,5]{1,2,0:T(8,128)(2,1)S(1)} all-gather(bf16[1,32,5]{1,2,0:T(8,128)(2,1)S(1)} %maximum_bitcast_fusion.1), channel_id=1, replica_groups=mesh['dp'=8,'fsdp'=4] {'dp','fsdp'}, dimensions={0}, use_global_device_ids=true | all-gather | bytes 10560 | tf_op jit(solution)/shard_map/all_gather | solution.py:111
  91.6 8.7 %all_gather.30 = bf16[256,1024]{1,0:T(8,128)(2,1)S(1)} all-gather(bf16[32,1024]{1,0:T(8,128)(2,1)S(1)} %copy-done.14), channel_id=1, replica_groups=mesh['dp'=8,'fsdp'=4] {'dp'}, dimensions={0}, use_global_device_ids=true | all-gather | bytes 589824 | tf_op jit(solution)/shard_map/all_gather | solution.py:83
  102.1 2.8 fusion.29
  107.1 29.1 %all_to_all.41 = bf16[4,128,1024]{2,1,0:T(8,128)(2,1)S(1)} all-to-all(bf16[4,128,1024]{2,1,0:T(8,128)(2,1)S(1)} %bitcast.163), channel_id=1, replica_groups=mesh['dp'=8,'fsdp'=4] {'fsdp'}, dimensions={0} | all-to-all | bytes 2097152 | tf_op jit(solution)/shard_map/all_to_all | solution.py:60
  141.4 2.6 reshape.252
  147.4 29.2 %all_to_all.42 = bf16[4,32,2304]{2,1,0:T(8,128)(2,1)} all-to-all(bf16[4,32,2304]{2,1,0:T(8,128)(2,1)S(1)} %pad_maximum_fusion.6), channel_id=1, replica_groups=mesh['dp'=8,'fsdp'=4] {'fsdp'}, dimensions={0} | all-to-all | bytes 1179648 | tf_op jit(solution)/shard_map/all_to_all | solution.py:79
  178.1 37.2 %all-gather.15.cloned.1.call-done = bf16[1024,2304]{1,0:T(8,128)(2,1)} async-done(((bf16[128,2304]{1,0:T(8,128)(2,1)}), bf16[1024,2304]{1,0:T(8,128)(2,1)}) %all-gather.15.cloned.1.call-update) | async-done | bytes 4718608 | tf_op jit(solution)/shard_map/all_gather | solution.py:83
  215.3 7.4 %fusion.38 = f32[512,2304]{1,0:T(8,128)} fusion(bf16[512,1024]{1,0:T(8,128)(2,1)} %all-gather.13.cloned.1.call-done, bf16[1024,2304]{1,0:T(8,128)(2,1)} %all-gather.15.cloned.1.call-done), kind=kOutput, calls=%fused_computation.95 | convolution fusion | flops 2415919104 | bytes 10485760 | tf_op jit(solution)/shard_map/dot_general | solution.py:15
  222.7 22.0 %all-gather.23.cloned.1.call-done = bf16[1,512,1024]{2,1,0:T(8,128)(2,1)} async-done(((bf16[1,128,1024]{2,1,0:T(8,128)(2,1)}), bf16[1,512,1024]{2,1,0:T(8,128)(2,1)}) %all-gather.23.cloned.1.call-update) | async-done | bytes 1048592 | tf_op jit(solution)/shard_map/all_gather | solution.py:53
  244.7 30.0 %all-gather.17.cloned.1.call-done = bf16[1152,1024]{1,0:T(8,128)(2,1)} async-done(((bf16[144,1024]{1,0:T(8,128)(2,1)}), bf16[1152,1024]{1,0:T(8,128)(2,1)}) %all-gather.17.cloned.1.call-update) | async-done | bytes 2359312 | tf_op jit(solution)/shard_map/all_gather | solution.py:83
  274.8 6.9 multiply_convert_fusion.1
  281.7 2.6 fusion.5
  284.3 30.7 %all_to_all.43 = bf16[4,128,1024]{2,1,0:T(8,128)(2,1)S(1)} all-to-all(bf16[4,128,1024]{2,1,0:T(8,128)(2,1)S(1)} %bitcast.173), channel_id=1, replica_groups=mesh['dp'=8,'fsdp'=4] {'fsdp'}, dimensions={0} | all-to-all | bytes 2097152 | tf_op jit(solution)/shard_map/all_to_all | solution.py:60
  316.5 26.2 %all-gather.19.cloned.1.call-done = bf16[512,1024]{1,0:T(8,128)(2,1)} async-done(((bf16[128,1024]{1,0:T(8,128)(2,1)}), bf16[512,1024]{1,0:T(8,128)(2,1)}) %all-gather.19.cloned.1.call-update) | async-done | bytes 1048592 | tf_op jit(solution)/shard_map/all_gather | solution.py:53
  346.2 2.8 fusion.27
  350.2 6.8 fusion.3
  358.1 3.6 convolution_convert_fusion
  361.7 4.2 all-to-all-start.5
  366.6 24.9 %all-to-all-done.5 = bf16[4,128,1024]{2,1,0:T(8,128)(2,1)} async-done(((bf16[4,128,1024]{2,1,0:T(8,128)(2,1)}), bf16[4,128,1024]{2,1,0:T(8,128)(2,1)}, u32[]{:S(2)}, u32[]{:S(2)}) %all-to-all-start.5) | async-done | bytes 1048608 | tf_op jit(solution)/shard_map/all_to_all | solution.py:60
  396.1 5.2 fusion.6
  402.5 4.8 convolution_convert_fusion.1
  407.4 3.5 all-to-all-start.3
  412.7 22.9 %all-to-all-done.3 = bf16[4,128,1024]{2,1,0:T(8,128)(2,1)S(1)} async-done(((bf16[4,128,1024]{2,1,0:T(8,128)(2,1)}), bf16[4,128,1024]{2,1,0:T(8,128)(2,1)S(1)}, u32[]{:S(2)}, u32[]{:S(2)}) %all-to-all-start.3) | async-done | bytes 1048608 | tf_op jit(solution)/shard_map/all_to_all | solution.py:60
  435.5 3.4 all-to-all-start.6
  438.9 36.0 %reduce-scatter.12.cloned.1.call-done = f32[128,2304]{1,0:T(8,128)} async-done(((f32[1024,2304]{1,0:T(8,128)}), f32[128,2304]{1,0:T(8,128)}) %reduce-scatter.12.cloned.1.call-update) | async-done | bytes 1179664 | tf_op jit(solution)/shard_map/reduce_scatter | solution.py:87
  475.0 2.1 convert_element_type.116
  477.1 4.6 all-to-all-start.7
  483.2 130.8 %reduce-scatter.16.cloned.1.call-done = f32[32,5]{1,0:T(8,128)} async-done(((f32[1024,5]{1,0:T(8,128)}), f32[32,5]{1,0:T(8,128)}) %reduce-scatter.16.cloned.1.call-update) | async-done | bytes 656
  618.9 2.1 reshape.270
  628.4 21.6 %reduce-scatter.10.cloned.1.call-done = f32[32,1024]{1,0:T(8,128)} async-done(((f32[256,1024]{1,0:T(8,128)}), f32[32,1024]{1,0:T(8,128)}) %reduce-scatter.10.cloned.1.call-update) | async-done | bytes 131088 | tf_op jit(solution)/shard_map/reduce_scatter | solution.py:87
  650.0 57.7 %reduce-scatter.14.cloned.1.call-done = f32[144,1024]{1,0:T(8,128)} async-done(((f32[1152,1024]{1,0:T(8,128)}), f32[144,1024]{1,0:T(8,128)}) %reduce-scatter.14.cloned.1.call-update) | async-done | bytes 589840 | tf_op jit(solution)/shard_map/reduce_scatter | solution.py:87
  (147 shorter events, 46.5 us)
Async XLA Ops:
  7.2 93.2 %all-gather.21.cloned.1.call-start = ((), (), s32[]{:S(2)}) async-start(), calls=%async_computation.22 | async-start | bytes 1310720 | tf_op jit(solution)/shard_map/all_gather | solution.py:53
  7.9 16.2 %copy-start.15 = (bf16[3,32]{1,0:T(4,128)(2,1)S(1)}, bf16[3,32]{1,0:T(4,128)(2,1)}, u32[]{:S(2)}) copy-start(bf16[3,32]{1,0:T(4,128)(2,1)} %param.13) | copy-start | bytes 580
  7.9 16.2 %copy-start.16 = (bf16[32]{0:T(256)(128)(2,1)S(1)}, bf16[32]{0:T(256)(128)(2,1)}, u32[]{:S(2)}) copy-start(bf16[32]{0:T(256)(128)(2,1)} %param.15) | copy-start | bytes 196
  7.9 16.2 %copy-start.17 = (bf16[32]{0:T(256)(128)(2,1)S(1)}, bf16[32]{0:T(256)(128)(2,1)}, u32[]{:S(2)}) copy-start(bf16[32]{0:T(256)(128)(2,1)} %param.11) | copy-start | bytes 196
  7.9 83.7 %copy-start.14 = (bf16[32,1024]{1,0:T(8,128)(2,1)S(1)}, bf16[32,1024]{1,0:T(8,128)(2,1)}, u32[]{:S(2)}) copy-start(bf16[32,1024]{1,0:T(8,128)(2,1)} %param.14) | copy-start | bytes 196612
  8.0 94.1 %all-gather.11.cloned.1.call-start = ((), (), s32[]{:S(2)}) async-start(), calls=%async_computation.13 | async-start | bytes 1769472 | tf_op jit(solution)/shard_map/all_gather | solution.py:83
  24.0 154.1 %all-gather.13.cloned.1.call-start = ((), (), s32[]{:S(2)}) async-start(), calls=%async_computation.14 | async-start | bytes 1310720 | tf_op jit(solution)/shard_map/all_gather | solution.py:53
  100.3 5.6 copy-start.1
  107.1 29.3 %copy-start = (bf16[1,128,1024]{2,1,0:T(8,128)(2,1)S(1)}, bf16[1,128,1024]{2,1,0:T(8,128)(2,1)}, u32[]{:S(2)}) copy-start(bf16[1,128,1024]{2,1,0:T(8,128)(2,1)} %param.10) | copy-start | bytes 786436
  136.2 1.3 copy-start.9
  137.4 77.9 %all-gather.15.cloned.1.call-start = ((), (), s32[]{:S(2)}) async-start(), calls=%async_computation.15 | async-start | bytes 5308416 | tf_op jit(solution)/shard_map/all_gather | solution.py:83
  176.6 68.1 %all-gather.23.cloned.1.call-start = ((), (), s32[]{:S(2)}) async-start(), calls=%async_computation.23 | async-start | bytes 1310720 | tf_op jit(solution)/shard_map/all_gather | solution.py:53
  177.2 97.5 %all-gather.17.cloned.1.call-start = ((), (), s32[]{:S(2)}) async-start(), calls=%async_computation.16 | async-start | bytes 2654208 | tf_op jit(solution)/shard_map/all_gather | solution.py:83
  177.8 164.9 %all-gather.19.cloned.1.call-start = ((), (), s32[]{:S(2)}) async-start(), calls=%async_computation.17 | async-start | bytes 1310720 | tf_op jit(solution)/shard_map/all_gather | solution.py:53
  274.8 6.9 copy-start.18
  281.6 2.6 copy-start.20
  281.7 2.7 copy-start.21
  284.3 31.1 %copy-start.3 = (bf16[1,128,1024]{2,1,0:T(8,128)(2,1)S(1)}, bf16[1,128,1024]{2,1,0:T(8,128)(2,1)}, u32[]{:S(2)}) copy-start(bf16[1,128,1024]{2,1,0:T(8,128)(2,1)} %param.19) | copy-start | bytes 786436
  316.4 94.5 %reduce-scatter.8.cloned.1.call-start = ((), (), s32[]{:S(2)}) async-start(), calls=%async_computation.18 | async-start | bytes 3538944 | tf_op jit(solution)/shard_map/reduce_scatter | solution.py:87
  344.9 1.3 copy-start.8
  349.0 125.9 %reduce-scatter.12.cloned.1.call-start = ((), (), s32[]{:S(2)}) async-start(), calls=%async_computation.20 | async-start | bytes 10616832 | tf_op jit(solution)/shard_map/reduce_scatter | solution.py:87
  361.7 29.8 %all-to-all-start.5 = ((bf16[4,128,1024]{2,1,0:T(8,128)(2,1)}), bf16[4,128,1024]{2,1,0:T(8,128)(2,1)}, u32[]{:S(2)}, u32[]{:S(2)}) async-start(bf16[4,128,1024]{2,1,0:T(8,128)(2,1)} %bitcast.23), calls=%async_computation.5 | async-start | bytes 2097152 | tf_op jit(solution)/shard_map/all_to_all | solution.py:60
  365.9 28.6 %copy-start.2 = (bf16[512,1024]{1,0:T(8,128)(2,1)S(1)}, bf16[512,1024]{1,0:T(8,128)(2,1)}, u32[]{:S(2)}) copy-start(bf16[512,1024]{1,0:T(8,128)(2,1)} %all-gather.19.cloned.1.call-done) | copy-start | bytes 3145732
  365.9 28.6 %copy-start.6 = (bf16[512,256]{1,0:T(8,128)(2,1)S(1)}, bf16[512,256]{1,0:T(8,128)(2,1)}, u32[]{:S(2)}) copy-start(bf16[512,256]{1,0:T(8,128)(2,1)} %copy-done.5) | copy-start | bytes 786436
  365.9 248.0 %reduce-scatter.16.cloned.1.call-start = ((), (), s32[]{:S(2)}) async-start(), calls=%async_computation.24 | async-start | bytes 540672
  394.2 255.8 %reduce-scatter.10.cloned.1.call-start = ((), (), s32[]{:S(2)}) async-start(), calls=%async_computation.19 | async-start | bytes 1179648 | tf_op jit(solution)/shard_map/reduce_scatter | solution.py:87
  396.0 311.7 %reduce-scatter.14.cloned.1.call-start = ((), (), s32[]{:S(2)}) async-start(), calls=%async_computation.21 | async-start | bytes 5308416 | tf_op jit(solution)/shard_map/reduce_scatter | solution.py:87
  401.3 1.3 copy-start.7
  407.4 28.2 %all-to-all-start.3 = ((bf16[4,128,1024]{2,1,0:T(8,128)(2,1)}), bf16[4,128,1024]{2,1,0:T(8,128)(2,1)S(1)}, u32[]{:S(2)}, u32[]{:S(2)}) async-start(bf16[4,128,1024]{2,1,0:T(8,128)(2,1)} %bitcast.172), calls=%async_computation.3 | async-start | bytes 2097152 | tf_op jit(solution)/shard_map/all_to_all | solution.py:60
  435.5 41.6 %all-to-all-start.6 = ((bf16[4,32,768]{2,1,0:T(8,128)(2,1)}), bf16[4,32,768]{2,1,0:T(8,128)(2,1)S(1)}, u32[]{:S(2)}, u32[]{:S(2)}) async-start(bf16[4,32,768]{2,1,0:T(8,128)(2,1)} %bitcast.29), calls=%async_computation.7 | async-start | bytes 393216 | tf_op jit(solution)/shard_map/all_to_all | solution.py:79
  438.9 43.0 %copy-start.4 = (bf16[1,128,1024]{2,1,0:T(8,128)(2,1)S(1)}, bf16[1,128,1024]{2,1,0:T(8,128)(2,1)}, u32[]{:S(2)}) copy-start(bf16[1,128,1024]{2,1,0:T(8,128)(2,1)} %param.19) | copy-start | bytes 786436
  477.1 143.9 %all-to-all-start.7 = ((bf16[4,32,2304]{2,1,0:T(8,128)(2,1)}), bf16[4,32,2304]{2,1,0:T(8,128)(2,1)}, u32[]{:S(2)}, u32[]{:S(2)}) async-start(bf16[4,32,2304]{2,1,0:T(8,128)(2,1)} %bitcast.167), calls=%async_computation.10 | async-start | bytes 1179648 | tf_op jit(solution)/shard_map/all_to_all | solution.py:79
  (6 other events, 5.4 us)
Sparse Core Ops, SparseCore 0:
  9.6 31.4 all-gather.20
  42.9 24.9 all-gather.10
  137.5 38.0 all-gather.12
  177.3 37.9 all-gather.14
  216.7 27.9 all-gather.22
  246.5 28.2 all-gather.16
  316.6 26.1 all-gather.18
  349.2 45.4 reduce-scatter.7
  398.1 76.8 reduce-scatter.11
  477.6 136.2 reduce-scatter.15
  617.7 32.2 reduce-scatter.9
  653.9 53.7 reduce-scatter.13

commit v2 on v1

--- a/solution.py
+++ b/solution.py
@@ -1,6 +1,10 @@
+import functools
+
 import jax
 import jax.numpy as jnp
 from jax import lax
+from jax.experimental import pallas as pl
+from jax.experimental.pallas import tpu as pltpu
 from jax.sharding import PartitionSpec as P
 
 KW = 3
@@ -8,7 +12,8 @@
 
 EPS = 1e-05
 
-GRAD = jnp.float32
+CORES = 2
+MESH = pl.DeviceIdType.MESH
 
 
 def product(left, right):
@@ -79,12 +84,204 @@
     return lax.all_to_all(blocks, "fsdp", split_axis=0, concat_axis=0, tiled=True)
 
 
-def gather_dp(rows):
-    return lax.all_gather(rows, "dp", axis=0, tiled=True)
-
-
-def reduce_dp(partial_grad):
-    return lax.psum_scatter(partial_grad, "dp", scatter_dimension=0, tiled=True)
+def greet(peers):
+    barrier = pltpu.get_barrier_semaphore()
+    for peer in peers:
+        pl.semaphore_signal(barrier, inc=1, device_id=peer, device_id_type=MESH)
+    pl.semaphore_wait(barrier, len(peers))
+
+
+def push(src, dst, sends, recvs, index, peer):
+    copy = pltpu.make_async_remote_copy(
+        src_ref=src,
+        dst_ref=dst,
+        send_sem=sends.at[index],
+        recv_sem=recvs.at[index],
+        device_id=peer,
+        device_id_type=MESH,
+    )
+    copy.start()
+    return copy
+
+
+def place():
+    dp, fs = lax.axis_index("dp"), lax.axis_index("fsdp")
+    pair, core = dp // CORES, lax.rem(dp, CORES)
+    return dp, fs, pair, core, (pair * CORES + 1 - core, fs)
+
+
+def gather_kernel(
+    pairs, fs_count,
+    x_ref, cot_ref, small_ref, in_ref, gu_ref, out_ref, down_ref,
+    x_all, cot_all, small_all, in_all, gu_all, out_all, down_all,
+    local_sem, z_send, z_recv, p_send, p_recv, c_send, c_recv,
+):
+    dp, fs, pair, core, partner = place()
+    z_peers = [(dp, lax.rem(fs + o, fs_count)) for o in range(1, fs_count)]
+    p_peers = [(lax.rem(pair + o, pairs) * CORES + core, fs) for o in range(1, pairs)]
+    p_from = [lax.rem(pair + pairs - o, pairs) * CORES + core for o in range(1, pairs)]
+    greet(z_peers + p_peers + [partner])
+    spread = [small_all, in_all, gu_all, out_all, down_all]
+
+    across = [[None] * len(p_peers) for _ in spread]
+    twins = [[None] * pairs for _ in spread]
+
+    def spread_own(kind, src):
+        dst = spread[kind].at[dp]
+        for o, peer in enumerate(p_peers):
+            across[kind][o] = push(src, dst, p_send, p_recv, (kind, o), peer)
+        twins[kind][0] = push(src, dst, c_send, c_recv, (kind, 0), partner)
+
+    along = [[], [], [], [], []]
+    for o, peer in enumerate(z_peers):
+        to = peer[1]
+        along[0].append(push(small_ref, small_all.at[dp, fs], z_send, z_recv, (0, o), peer))
+        along[1].append(push(in_ref.at[to], in_all.at[dp, fs], z_send, z_recv, (1, o), peer))
+    for o, peer in enumerate(z_peers):
+        to = peer[1]
+        along[2].append(push(gu_ref.at[to], gu_all.at[dp, fs], z_send, z_recv, (2, o), peer))
+    for o, peer in enumerate(z_peers):
+        along[3].append(push(x_ref, x_all.at[fs], z_send, z_recv, (3, o), peer))
+    for o, peer in enumerate(z_peers):
+        along[4].append(push(cot_ref, cot_all.at[fs], z_send, z_recv, (4, o), peer))
+    spread_own(3, out_ref)
+    spread_own(4, down_ref)
+    local = []
+    for index, (src, dst) in enumerate(
+        [
+            (small_ref, small_all.at[dp, fs]),
+            (in_ref.at[fs], in_all.at[dp, fs]),
+            (gu_ref.at[fs], gu_all.at[dp, fs]),
+            (x_ref, x_all.at[fs]),
+            (cot_ref, cot_all.at[fs]),
+            (out_ref, out_all.at[dp]),
+            (down_ref, down_all.at[dp]),
+        ]
+    ):
+        copy = pltpu.make_async_copy(src, dst, local_sem.at[index])
+        copy.start()
+        local.append(copy)
+    for kind in range(3):
+        local[kind].wait()
+        for copy in along[kind]:
+            copy.wait_recv()
+        spread_own(kind, spread[kind].at[dp])
+    for kind in (3, 0, 1, 4, 2):
+        for o, source in enumerate(p_from):
+            across[kind][o].wait_recv()
+            block = spread[kind].at[source]
+            twins[kind][o + 1] = push(block, block, c_send, c_recv, (kind, o + 1), partner)
+    for copy in local[3:]:
+        copy.wait()
+    for copy in along[3] + along[4]:
+        copy.wait_recv()
+    for row in along + across:
+        for copy in row:
+            copy.wait_send()
+    for row in twins:
+        for copy in row:
+            copy.wait()
+
+
+def gather_all(x, cot, small, in_blocks, gu_blocks, out_shard, down_shard):
+    dp_count, fs_count = lax.axis_size("dp"), lax.axis_size("fsdp")
+    pairs = dp_count // CORES
+    arrays = (x, cot, small, in_blocks, gu_blocks, out_shard, down_shard)
+    shapes = (
+        (fs_count,) + x.shape,
+        (fs_count,) + cot.shape,
+        (dp_count, fs_count) + small.shape,
+        (dp_count,) + in_blocks.shape,
+        (dp_count,) + gu_blocks.shape,
+        (dp_count,) + out_shard.shape,
+        (dp_count,) + down_shard.shape,
+    )
+    return pl.pallas_call(
+        functools.partial(gather_kernel, pairs, fs_count),
+        out_shape=[jax.ShapeDtypeStruct(shape, x.dtype) for shape in shapes],
+        in_specs=[pl.BlockSpec(memory_space=pltpu.VMEM)] * len(arrays),
+        out_specs=[pl.BlockSpec(memory_space=pl.ANY)] * len(shapes),
+        scratch_shapes=[
+            pltpu.SemaphoreType.DMA((7,)),
+            pltpu.SemaphoreType.DMA((5, fs_count - 1)),
+            pltpu.SemaphoreType.DMA((5, fs_count - 1)),
+            pltpu.SemaphoreType.DMA((5, pairs - 1)),
+            pltpu.SemaphoreType.DMA((5, pairs - 1)),
+            pltpu.SemaphoreType.DMA((5, pairs)),
+            pltpu.SemaphoreType.DMA((5, pairs)),
+        ],
+        compiler_params=pltpu.CompilerParams(collective_id=0, has_side_effects=True),
+        name="gather_all",
+    )(*arrays)
+
+
+def twin_kernel(count, pairs, *refs):
+    partials, received = refs[:count], refs[count : 2 * count]
+    sends, recvs = refs[2 * count :]
+    _, _, _, core, partner = place()
+    greet([partner])
+    copies = [
+        push(partial.at[j, 1 - core], landed.at[j], sends, recvs, (k, j), partner)
+        for k, (partial, landed) in enumerate(zip(partials, received))
+        for j in range(pairs)
+    ]
+    for copy in copies:
+        copy.wait()
+
+
+def pair_kernel(count, pairs, *refs):
+    partials, received = refs[:count], refs[count : 2 * count]
+    sends, recvs = refs[2 * count :]
+    _, fs, pair, core, _ = place()
+    targets = [lax.rem(pair + o, pairs) for o in range(1, pairs)]
+    peers = [(to * CORES + core, fs) for to in targets]
+    greet(peers)
+    copies = [
+        push(partial.at[to], landed.at[o], sends, recvs, (k, o), peer)
+        for k, (partial, landed) in enumerate(zip(partials, received))
+        for o, (to, peer) in enumerate(zip(targets, peers))
+    ]
+    for copy in copies:
+        copy.wait()
+
+
+def exchange_call(kernel, partials, slots, collective_id, name):
+    count = len(partials)
+    pairs = lax.axis_size("dp") // CORES
+    return pl.pallas_call(
+        functools.partial(kernel, count, pairs),
+        out_shape=[jax.ShapeDtypeStruct((slots,) + p.shape[-2:], p.dtype) for p in partials],
+        in_specs=[pl.BlockSpec(memory_space=pl.ANY)] * count,
+        out_specs=[pl.BlockSpec(memory_space=pl.ANY)] * count,
+        scratch_shapes=[pltpu.SemaphoreType.DMA((count, slots))] * 2,
+        compiler_params=pltpu.CompilerParams(collective_id=collective_id, has_side_effects=True),
+        name=name,
+    )(*partials)
+
+
+def reduce_all(partials):
+    dp_count = lax.axis_size("dp")
+    pairs = dp_count // CORES
+    dp = lax.axis_index("dp")
+    core, pair = lax.rem(dp, CORES), dp // CORES
+    split = [
+        p.astype(jnp.bfloat16).reshape(pairs, CORES, p.shape[0] // dp_count, p.shape[1])
+        for p in partials
+    ]
+    landed = exchange_call(twin_kernel, split, pairs, 1, "twin_exchange")
+    chip = [
+        (
+            lax.dynamic_index_in_dim(p, core, axis=1, keepdims=False).astype(jnp.float32)
+            + r.astype(jnp.float32)
+        ).astype(jnp.bfloat16)
+        for p, r in zip(split, landed)
+    ]
+    others = exchange_call(pair_kernel, chip, pairs - 1, 2, "pair_exchange")
+    return [
+        lax.dynamic_index_in_dim(p, pair, axis=0, keepdims=False).astype(jnp.float32)
+        + jnp.sum(r.astype(jnp.float32), axis=0)
+        for p, r in zip(chip, others)
+    ]
 
 
 def split_features(
@@ -106,33 +303,41 @@
     quarter = dp_count * part
     hid = dp_count * weight_down.shape[0]
 
-    x_all = whole_sequence(inputs[0])
     small = jnp.concatenate([gain_mixer[None], gain_ffn[None], conv_taps], axis=0)
-    small_all = lax.all_gather(small, ("dp", "fsdp"), axis=1, tiled=True)
-    gain1, gain2 = small_all[0], small_all[1]
-    taps32 = lax.dynamic_index_in_dim(
-        small_all[2:].reshape(KW, dp_count, fs_count, part),
-        lax.axis_index("fsdp"),
+    lanes = max(128, part)
+    small = jnp.pad(small, ((0, 8 - small.shape[0]), (0, lanes - part)))
+    gu_blocks = jnp.concatenate(
+        [
+            column_blocks(weight_gate, 1, dp_count, fs_count),
+            column_blocks(weight_up, 1, dp_count, fs_count),
+        ],
         axis=2,
-        keepdims=False,
-    ).reshape(KW, quarter).astype(jnp.float32)
-
-    in_blocks = exchange(column_blocks(weight_in, 3, dp_count, fs_count))
-    gu_blocks = exchange(
-        jnp.concatenate(
-            [
-                column_blocks(weight_gate, 1, dp_count, fs_count),
-                column_blocks(weight_up, 1, dp_count, fs_count),
-            ],
-            axis=2,
-        )
-    )
-    in_cols = gather_dp(in_blocks.reshape(fs_count * part, 3 * quarter))
-    out_rows = gather_dp(weight_out)
-    gu_cols = gather_dp(gu_blocks.reshape(fs_count * part, 2 * hid))
-    down_rows = gather_dp(weight_down)
+    )
     grad_out = cotangent[0]
-    grad_all = whole_sequence(grad_out)
+    x_all, grad_all, small_all, in_cols, gu_cols, out_rows, down_rows = gather_all(
+        inputs[0],
+        grad_out,
+        small,
+        column_blocks(weight_in, 3, dp_count, fs_count),
+        gu_blocks,
+        weight_out,
+        weight_down,
+    )
+    x_all = x_all.reshape(-1, width)
+    grad_all = grad_all.reshape(-1, width)
+    in_cols = in_cols.reshape(width, 3 * quarter)
+    gu_cols = gu_cols.reshape(width, 2 * hid)
+    out_rows = out_rows.reshape(quarter, width)
+    down_rows = down_rows.reshape(hid, width)
+    small_all = small_all[:, :, : KW + 2, :part]
+    gain1 = small_all[:, :, 0].reshape(width)
+    gain2 = small_all[:, :, 1].reshape(width)
+    taps32 = (
+        lax.dynamic_index_in_dim(small_all, lax.axis_index("fsdp"), axis=1, keepdims=False)[:, 2:]
+        .transpose(1, 0, 2)
+        .reshape(KW, quarter)
+        .astype(jnp.float32)
+    )
 
     _, _, pre1_all = norm_forward(x_all.astype(jnp.float32), gain1)
     act1_all = pre1_all.astype(jnp.bfloat16)
@@ -161,8 +366,6 @@
     dgu = jnp.concatenate([dgate, dupval], axis=1)
     dact3 = token_share(product_nt(dgu, gu_cols))
     outputs = (resid + token_share(product(act4, down_rows))).astype(jnp.bfloat16)
-    g_gu = reduce_dp(product_tn(act3_all, dgu).astype(GRAD))
-    g_down = reduce_dp(product_tn(act4, grad_all).astype(GRAD))
     dnorm2, g_gain2 = norm_backward(dact3, normed2, scale2, gain2)
     dresid = grad_out.astype(jnp.float32) + dnorm2
     dres_all = whole_sequence(dresid.astype(jnp.bfloat16))
@@ -177,13 +380,21 @@
         dgated = dgated + taps32[offset] * leading(dconv, offset)
     dproj = jnp.concatenate([dgated * xpart, dcpart, dgated * bpart], axis=1).astype(jnp.bfloat16)
     dact1 = token_share(product_nt(dproj, in_cols))
-    g_in = reduce_dp(product_tn(act1_all, dproj).astype(GRAD))
-    g_out = reduce_dp(product_tn(act2, dres_all).astype(GRAD))
+    g_gu, g_down, g_in, g_out = reduce_all(
+        [
+            product_tn(act3_all, dgu),
+            product_tn(act4, grad_all),
+            product_tn(act1_all, dproj),
+            product_tn(act2, dres_all),
+        ]
+    )
     dnorm1, g_gain1 = norm_backward(dact1, normed1, scale1, gain1)
     grad_inputs = dresid + dnorm1
 
-    g_gu_owned = exchange(g_gu.reshape(fs_count, part, 2 * hid).astype(jnp.bfloat16)).astype(jnp.float32)
-    g_in_owned = exchange(g_in.reshape(fs_count, part, 3 * quarter).astype(jnp.bfloat16)).astype(jnp.float32)
+    moved = jnp.concatenate([g_in, g_gu], axis=1).astype(jnp.bfloat16)
+    moved = exchange(moved.reshape(fs_count, part, 3 * quarter + 2 * hid)).astype(jnp.float32)
+    g_in_owned = moved[:, :, : 3 * quarter]
+    g_gu_owned = moved[:, :, 3 * quarter :]
     own_column = (jnp.arange(fs_count) == lax.axis_index("fsdp"))[None, None, :, None]
     taps_spread = jnp.where(own_column, g_taps.reshape(KW, dp_count, 1, part), 0.0).reshape(KW, width)
     small_owned = lax.psum_scatter(
@@ -198,11 +409,11 @@
         small_owned[0],
         column_join(g_in_owned, 3, dp_count, fs_count),
         small_owned[2:],
-        g_out.astype(jnp.float32),
+        g_out,
         small_owned[1],
         column_join(g_gu_owned[:, :, :hid], 1, dp_count, fs_count),
         column_join(g_gu_owned[:, :, hid:], 1, dp_count, fs_count),
-        g_down.astype(jnp.float32),
+        g_down,
     )
 
 

time: 716 us -> 526 us (0.73)
  waiting for transfers between devices: 411 us -> 227 us
  blocking collectives: 179 us -> 28.6 us
  Pallas kernels: 0 us -> 129 us
  other arithmetic: 13.8 us -> 34 us
  matrix products: 46.8 us -> 36 us
    pallas_call x0 -> x3, Pallas kernels: none -> 129 us  [the longest x1 67.1 us: gather_all(): pl.pallas_call(functools.partial(gather_kernel, pairs, fs_count), out_sha...]
    reduce_scatter x4 -> x0, waiting for transfers between devices: 115 us -> none  [reduce_dp(): return lax.psum_scatter(partial_grad, 'dp', scatter_dimension=0, tiled=True)]
    all_gather x2 -> x0, blocking collectives: 75.7 us -> none  [the longest x1 67 us: split_features(): small_all = lax.all_gather(small, ('dp', 'fsdp'), axis=1, tiled=True)]
    all_gather x3 -> x0, waiting for transfers between devices: 67.3 us -> none  [gather_dp(): return lax.all_gather(rows, 'dp', axis=0, tiled=True)]
    all_to_all x2 -> x0, blocking collectives: 43.1 us -> none  [exchange(): lax.all_to_all(blocks, 'fsdp', split_axis=0, concat_axis=0, tiled=True)]
    all_to_all x2 -> x1, blocking collectives: 59.7 us -> 28.6 us  [token_share(): lax.all_to_all(pieces, 'fsdp', split_axis=0, concat_axis=0, tiled=True)]
    all_to_all x2 -> x3, waiting for transfers between devices: 47.7 us -> 25.9 us  [token_share(): lax.all_to_all(pieces, 'fsdp', split_axis=0, concat_axis=0, tiled=True)]
    all_to_all x2 -> x1, waiting for transfers between devices: 0.01 us -> 13.8 us  [exchange(): lax.all_to_all(blocks, 'fsdp', split_axis=0, concat_axis=0, tiled=True)]
  transfers between devices with their start and end apart: 16 -> 7, of which waited for: 10 -> 6; matrix products, arithmetic and copies ran while one was open for 9% -> 13% of each run, Pallas kernels for 0% -> 12%
where the time goes in v2:
time: 526 us; the launch traced here: 525 us
  waiting for transfers between devices  227 us (43%)
  Pallas kernels  129 us (25%)
  local copies, waits for them, and re-layouts  36.2 us (7%)
  matrix products  36 us (7%)
  other arithmetic  34 us (6%)
  blocking collectives  28.6 us (5%)
  starting transfers between devices  20 us (4%)
  between operations  14.4 us (3%)
    unnamed x4, waiting for transfers between devices  134 us
    pallas_call x1, Pallas kernels, gather_all(): pl.pallas_call(functools.partial(gather_kernel, pairs, fs_count), out_sha...  67.1 us
    pallas_call x2, Pallas kernels, exchange_call(): pl.pallas_call(functools.partial(kernel, count, pairs), out_shape=[jax.Sh...  61.5 us
    all_gather x2, waiting for transfers between devices, whole_sequence(): return lax.all_gather(rows, 'fsdp', axis=0, tiled=True)  52.9 us
    all_to_all x1, blocking collectives, token_share(): lax.all_to_all(pieces, 'fsdp', split_axis=0, concat_axis=0, tiled=True)  28.6 us
    all_to_all x3, waiting for transfers between devices, token_share(): lax.all_to_all(pieces, 'fsdp', split_axis=0, concat_axis=0, tiled=True)  25.9 us
    all_to_all x3, starting transfers between devices, token_share(): lax.all_to_all(pieces, 'fsdp', split_axis=0, concat_axis=0, tiled=True)  16 us
    all_to_all x1, waiting for transfers between devices, exchange(): lax.all_to_all(blocks, 'fsdp', split_axis=0, concat_axis=0, tiled=True)  13.8 us
  transfers between devices with their start and end apart: 7, of which 6 were waited for; matrix products, arithmetic and copies ran while one was open for 13% of the time, Pallas kernels for 12%

profile of v2, /device:TPU:0, one launch (start us, length us, event | category | flops | bytes accessed | tf_op | source)
XLA Modules:
  0.0 524.9 jit_solution(15006553016043859256)
XLA Ops:
  7.2 1.9 reshape.312
  14.4 67.1 %gather_all.1 = (bf16[4,128,1024]{2,1,0:T(8,128)(2,1)}, bf16[4,128,1024]{2,1,0:T(8,128)(2,1)}, bf16[8,4,8,128]{3,2,1,0:T(8,128)(2,1)}, bf16[8,4,32,768]{3,2,1,0:...) custom-call(bf16[128,1024]{1,0:T(8,128)(2,1)} %bitcast.168, ...), custom_call_target="tpu_custom_call" | custom-call | tf_op jit(solution)/shard_map/gather_all/pallas_call | solution.py:199
  91.1 7.3 %all-to-all-start = ((bf16[4,128,1024]{2,1,0:T(8,128)(2,1)}), bf16[4,128,1024]{2,1,0:T(8,128)(2,1)}, u32[]{:S(2)}, u32[]{:S(2)}) async-start(bf16[4,128,1024]{2,1,0:T(8,128)(2,1)} %bitcast.12), calls=%async_computation | async-start | bytes 2097152 | tf_op jit(solution)/shard_map/all_to_all | solution.py:65
  98.5 24.9 %all-to-all-done = bf16[4,128,1024]{2,1,0:T(8,128)(2,1)} async-done(((bf16[4,128,1024]{2,1,0:T(8,128)(2,1)}), bf16[4,128,1024]{2,1,0:T(8,128)(2,1)}, u32[]{:S(2)}, u32[]{:S(2)}) %all-to-all-start) | async-done | bytes 1048608 | tf_op jit(solution)/shard_map/all_to_all | solution.py:65
  126.1 27.4 %all-gather.3.cloned.1.call-done = bf16[512,1024]{1,0:T(8,128)(2,1)} async-done(((bf16[128,1024]{1,0:T(8,128)(2,1)}), bf16[512,1024]{1,0:T(8,128)(2,1)}) %all-gather.3.cloned.1.call-update) | async-done | bytes 1048592 | tf_op jit(solution)/shard_map/all_gather | solution.py:58
  153.5 5.4 %fusion.40 = f32[512,2304]{1,0:T(8,128)S(1)} fusion(bf16[512,1024]{1,0:T(8,128)(2,1)} %all-gather.3.cloned.1.call-done, bf16[1024,2304]{1,0:T(8,128)(2,1)} %bitcast.203), kind=kOutput, calls=%fused_computation.124 | convolution fusion | flops 2415919104 | bytes 10485760 | tf_op jit(solution)/shard_map/dot_general | solution.py:20
  159.0 3.4 multiply_convert_fusion.1
  162.4 2.6 fusion.6
  165.1 28.6 %all_to_all.25 = bf16[4,128,1024]{2,1,0:T(8,128)(2,1)S(1)} all-to-all(bf16[4,128,1024]{2,1,0:T(8,128)(2,1)S(1)} %bitcast.192), channel_id=1, replica_groups=mesh['dp'=8,'fsdp'=4] {'fsdp'}, dimensions={0} | all-to-all | bytes 2097152 | tf_op jit(solution)/shard_map/all_to_all | solution.py:65
  195.2 2.6 fusion.3
  197.8 4.2 convolution_convert_fusion.4
  202.0 4.5 all-to-all-start.1
  206.5 4.6 convolution_convert_fusion.1
  211.1 4.4 convolution_convert_fusion
  215.5 25.5 %all-gather.5.cloned.1.call-done = bf16[512,1024]{1,0:T(8,128)(2,1)} async-done(((bf16[128,1024]{1,0:T(8,128)(2,1)}), bf16[512,1024]{1,0:T(8,128)(2,1)}) %all-gather.5.cloned.1.call-update) | async-done | bytes 1048592 | tf_op jit(solution)/shard_map/all_gather | solution.py:58
  241.0 2.1 multiply_reduce_fusion.3
  244.4 2.2 convolution_convert_fusion.2
  247.9 8.3 %twin_exchange.1 = (bf16[4,128,2304]{2,1,0:T(8,128)(2,1)}, bf16[4,144,1024]{2,1,0:T(8,128)(2,1)}, bf16[4,128,768]{2,1,0:T(8,128)(2,1)}, bf16[4,32,1024]{2,1,0:T(8,128)(2,1)}) custom-call(bf16[4,2,128,2304]{3,2,1,0:T(8,128)(2,1)} %bitcast.169, bf16[4,2,144,1024]{3,2,1,0:T(8,128)(2,1)} %bitcast.172, bf16[4,2,128,768]{3,2,1,0:T(8,128)(2,1)} %bitcast.177, ...), custom_call_target="tpu_custom_call" | custom-call | tf_op jit(solution)/shard_map/twin_exchange/pallas_call | solution.py:251
  256.3 1.9 fusion.17.refs_3_
  258.1 3.1 fusion.1.refs_1_
  261.3 3.8 fusion.refs_0_
  266.1 53.2 %pair_exchange.1 = (bf16[3,128,2304]{2,1,0:T(8,128)(2,1)}, bf16[3,144,1024]{2,1,0:T(8,128)(2,1)}, bf16[3,128,768]{2,1,0:T(8,128)(2,1)}, bf16[3,32,1024]{2,1,0:T(8,128)(2,1)}) custom-call(bf16[4,128,2304]{2,1,0:T(8,128)(2,1)} %fusion.refs_0_, bf16[4,144,1024]{2,1,0:T(8,128)(2,1)} %fusion.1.refs_1_, bf16[4,128,768]{2,1,0:T(8,128)(2,1)} %copy-done.2, ...), custom_call_target="tpu_custom_call" | custom-call | tf_op jit(solution)/shard_map/pair_exchange/pallas_call | solution.py:251
  323.5 3.5 all-to-all-start.4
  327.2 2.3 convert_reduce_fusion.3
  329.6 3.4 convolution_convert_fusion.3
  333.0 13.8 %all-to-all-done.4 = bf16[4,32,3072]{2,1,0:T(8,128)(2,1)S(1)} async-done(((bf16[4,32,3072]{2,1,0:T(8,128)(2,1)}), bf16[4,32,3072]{2,1,0:T(8,128)(2,1)S(1)}, u32[]{:S(2)}, u32[]{:S(2)}) %all-to-all-start.4) | async-done | bytes 786464 | tf_op jit(solution)/shard_map/all_to_all | solution.py:84
  346.9 4.2 all-to-all-start.3
  359.7 3.0 reshape.334
  366.1 3.0 reshape.332
  369.6 2.2 copy.65
  371.7 3.7 reshape.330
  380.5 134.4 %reduce-scatter.4.cloned.1.call-done = f32[32,5]{1,0:T(8,128)} async-done(((f32[1024,5]{1,0:T(8,128)}), f32[32,5]{1,0:T(8,128)}) %reduce-scatter.4.cloned.1.call-update) | async-done | bytes 656
  (159 shorter events, 48.2 us)
Async XLA Ops:
  7.2 2.4 copy-start.16
  11.6 2.2 copy-start.21
  91.1 33.7 %copy-start = (bf16[1,128,1024]{2,1,0:T(8,128)(2,1)S(1)}, bf16[1,128,1024]{2,1,0:T(8,128)(2,1)}, u32[]{:S(2)}) copy-start(bf16[1,128,1024]{2,1,0:T(8,128)(2,1)} %param.10) | copy-start | bytes 786436
  91.1 32.3 %all-to-all-start = ((bf16[4,128,1024]{2,1,0:T(8,128)(2,1)}), bf16[4,128,1024]{2,1,0:T(8,128)(2,1)}, u32[]{:S(2)}, u32[]{:S(2)}) async-start(bf16[4,128,1024]{2,1,0:T(8,128)(2,1)} %bitcast.12), calls=%async_computation | async-start | bytes 2097152 | tf_op jit(solution)/shard_map/all_to_all | solution.py:65
  98.4 55.1 %all-gather.3.cloned.1.call-start = ((), (), s32[]{:S(2)}) async-start(), calls=%async_computation.6 | async-start | bytes 1310720 | tf_op jit(solution)/shard_map/all_gather | solution.py:58
  125.9 115.1 %all-gather.5.cloned.1.call-start = ((), (), s32[]{:S(2)}) async-start(), calls=%async_computation.7 | async-start | bytes 1310720 | tf_op jit(solution)/shard_map/all_gather | solution.py:58
  153.5 5.4 %copy-start.24 = (bf16[8,144,1024]{2,1,0:T(8,128)(2,1)S(1)}, bf16[8,144,1024]{2,1,0:T(8,128)(2,1)}, u32[]{:S(2)}) copy-start(bf16[8,144,1024]{2,1,0:T(8,128)(2,1)} %get-tuple-element.30) | copy-start | bytes 7077892
  153.5 5.4 %copy-start.26 = (bf16[4,128,1024]{2,1,0:T(8,128)(2,1)S(1)}, bf16[4,128,1024]{2,1,0:T(8,128)(2,1)}, u32[]{:S(2)}) copy-start(bf16[4,128,1024]{2,1,0:T(8,128)(2,1)} %get-tuple-element.31) | copy-start | bytes 3145732
  153.5 8.9 %slice-start = ((s8[4718592]{0:T(1024)(128)(4,1)}), s8[4194304]{0:T(1024)(128)(4,1)S(1)}, s32[]{:S(2)}) async-start(s8[4718592]{0:T(1024)(128)(4,1)} %bitcast.204), calls=%async_computation.9 | async-start | bytes 8388608
  159.0 3.4 slice-start.1
  162.4 2.7 copy-start.29
  162.4 2.7 copy-start.31
  165.1 29.1 %copy-start.6 = (bf16[1,128,1024]{2,1,0:T(8,128)(2,1)S(1)}, bf16[1,128,1024]{2,1,0:T(8,128)(2,1)}, u32[]{:S(2)}) copy-start(bf16[1,128,1024]{2,1,0:T(8,128)(2,1)} %param.19) | copy-start | bytes 786436
  195.2 2.6 copy-start.28
  202.0 121.5 %all-to-all-start.1 = ((bf16[4,128,1024]{2,1,0:T(8,128)(2,1)}), bf16[4,128,1024]{2,1,0:T(8,128)(2,1)}, u32[]{:S(2)}, u32[]{:S(2)}) async-start(bf16[4,128,1024]{2,1,0:T(8,128)(2,1)} %bitcast.191), calls=%async_computation.1 | async-start | bytes 2097152 | tf_op jit(solution)/shard_map/all_to_all | solution.py:65
  206.5 4.6 copy-start.27
  206.5 4.6 copy-start.30
  206.5 4.6 copy-start.32
  244.4 2.2 copy-start.1
  244.4 2.2 copy-start.9
  247.9 8.4 %copy-start.4 = (bf16[256,1024]{1,0:T(8,128)(2,1)S(1)}, bf16[256,1024]{1,0:T(8,128)(2,1)}, u32[]{:S(2)}) copy-start(bf16[256,1024]{1,0:T(8,128)(2,1)} %convolution_convert_fusion.6) | copy-start | bytes 1572868
  256.2 5.0 copy-start.5
  261.3 3.8 copy-start.3
  261.3 3.8 copy-start.15
  322.5 7.2 %copy-start.18 = (bf16[512,256]{1,0:T(8,128)(2,1)S(1)}, bf16[512,256]{1,0:T(8,128)(2,1)}, u32[]{:S(2)}) copy-start(bf16[512,256]{1,0:T(8,128)(2,1)} %copy-done.17) | copy-start | bytes 786436
  323.5 23.4 %all-to-all-start.4 = ((bf16[4,32,3072]{2,1,0:T(8,128)(2,1)}), bf16[4,32,3072]{2,1,0:T(8,128)(2,1)S(1)}, u32[]{:S(2)}, u32[]{:S(2)}) async-start(bf16[4,32,3072]{2,1,0:T(8,128)(2,1)} %pad_maximum_fusion.6), calls=%async_computation.4 | async-start | bytes 1572864 | tf_op jit(solution)/shard_map/all_to_all | solution.py:84
  333.0 18.5 %copy-start.19 = (bf16[3,32,1024]{2,1,0:T(8,128)(2,1)S(1)}, bf16[3,32,1024]{2,1,0:T(8,128)(2,1)}, u32[]{:S(2)}) copy-start(bf16[3,32,1024]{2,1,0:T(8,128)(2,1)} %get-tuple-element.38) | copy-start | bytes 589828
  333.0 18.6 %copy-start.14 = (bf16[3,144,1024]{2,1,0:T(8,128)(2,1)S(1)}, bf16[3,144,1024]{2,1,0:T(8,128)(2,1)}, u32[]{:S(2)}) copy-start(bf16[3,144,1024]{2,1,0:T(8,128)(2,1)} %get-tuple-element.39) | copy-start | bytes 2654212
  346.9 29.6 %all-to-all-start.3 = ((bf16[4,128,1024]{2,1,0:T(8,128)(2,1)}), bf16[4,128,1024]{2,1,0:T(8,128)(2,1)}, u32[]{:S(2)}, u32[]{:S(2)}) async-start(bf16[4,128,1024]{2,1,0:T(8,128)(2,1)} %bitcast.21), calls=%async_computation.3 | async-start | bytes 2097152 | tf_op jit(solution)/shard_map/all_to_all | solution.py:65
  351.1 163.8 %reduce-scatter.4.cloned.1.call-start = ((), (), s32[]{:S(2)}) async-start(), calls=%async_computation.8 | async-start | bytes 540672
  375.4 3.9 copy-start.7
  375.4 3.9 copy-start.11
  (10 other events, 15.0 us)
Sparse Core Ops, SparseCore 0:
  126.0 27.4 all-gather.2
  195.3 45.6 all-gather.4
  379.4 135.4 reduce-scatter.3

commit v3 on v2

--- a/solution.py
+++ b/solution.py
@@ -54,18 +54,6 @@
     return jnp.concatenate([values[offset:], zeros], axis=0)
 
 
-def whole_sequence(rows):
-    return lax.all_gather(rows, "fsdp", axis=0, tiled=True)
-
-
-def token_share(partial_value):
-    fs_count = lax.axis_size("fsdp")
-    rows, columns = partial_value.shape
-    pieces = partial_value.astype(jnp.bfloat16).reshape(fs_count, rows // fs_count, columns)
-    received = lax.all_to_all(pieces, "fsdp", split_axis=0, concat_axis=0, tiled=True)
-    return jnp.sum(received.astype(jnp.float32), axis=0)
-
-
 def column_blocks(shard, lead, dp_count, fs_count):
     rows, columns = shard.shape
     inner = columns // (lead * dp_count * fs_count)
@@ -78,10 +66,6 @@
     inner = columns // (lead * dp_count)
     pieces = blocks.reshape(fs_count, rows, lead, dp_count, inner).transpose(1, 2, 3, 0, 4)
     return pieces.reshape(rows, lead * dp_count * fs_count * inner)
-
-
-def exchange(blocks):
-    return lax.all_to_all(blocks, "fsdp", split_axis=0, concat_axis=0, tiled=True)
 
 
 def greet(peers):
@@ -215,6 +199,70 @@
     )(*arrays)
 
 
+def line_kernel(count, fs_count, whole, *refs):
+    sources, landed = refs[:count], refs[count : 2 * count]
+    local_sem, sends, recvs = refs[2 * count :]
+    dp, fs, _, _, _ = place()
+    targets = [lax.rem(fs + o, fs_count) for o in range(1, fs_count)]
+    greet([(dp, to) for to in targets])
+    copies = [
+        push(src if whole else src.at[to], dst.at[fs], sends, recvs, (k, o), (dp, to))
+        for k, (src, dst) in enumerate(zip(sources, landed))
+        for o, to in enumerate(targets)
+    ]
+    local = []
+    for k, (src, dst) in enumerate(zip(sources, landed)):
+        copy = pltpu.make_async_copy(src if whole else src.at[fs], dst.at[fs], local_sem.at[k])
+        copy.start()
+        local.append(copy)
+    for copy in local + copies:
+        copy.wait()
+
+
+def along_line(arrays, whole, collective_id, name):
+    fs_count = lax.axis_size("fsdp")
+    count = len(arrays)
+    return pl.pallas_call(
+        functools.partial(line_kernel, count, fs_count, whole),
+        out_shape=[
+            jax.ShapeDtypeStruct(((fs_count,) + a.shape) if whole else a.shape, a.dtype)
+            for a in arrays
+        ],
+        in_specs=[pl.BlockSpec(memory_space=pltpu.VMEM)] * count,
+        out_specs=[pl.BlockSpec(memory_space=pl.ANY)] * count,
+        scratch_shapes=[
+            pltpu.SemaphoreType.DMA((count,)),
+            pltpu.SemaphoreType.DMA((count, fs_count - 1)),
+            pltpu.SemaphoreType.DMA((count, fs_count - 1)),
+        ],
+        compiler_params=pltpu.CompilerParams(collective_id=collective_id, has_side_effects=True),
+        name=name,
+    )(*arrays)
+
+
+def whole_sequence(rows, collective_id, name):
+    (received,) = along_line([rows], True, collective_id, name)
+    return received.reshape(-1, rows.shape[1])
+
+
+def token_pieces(partial_value):
+    fs_count = lax.axis_size("fsdp")
+    rows, columns = partial_value.shape
+    return partial_value.astype(jnp.bfloat16).reshape(fs_count, rows // fs_count, columns)
+
+
+def token_share(partial_value, collective_id, name):
+    (received,) = along_line([token_pieces(partial_value)], False, collective_id, name)
+    return jnp.sum(received.astype(jnp.float32), axis=0)
+
+
+def token_share_async(partial_value):
+    received = lax.all_to_all(
+        token_pieces(partial_value), "fsdp", split_axis=0, concat_axis=0, tiled=True
+    )
+    return jnp.sum(received.astype(jnp.float32), axis=0)
+
+
 def twin_kernel(count, pairs, *refs):
     partials, received = refs[:count], refs[count : 2 * count]
     sends, recvs = refs[2 * count :]
@@ -229,55 +277,83 @@
         copy.wait()
 
 
-def pair_kernel(count, pairs, *refs):
-    partials, received = refs[:count], refs[count : 2 * count]
-    sends, recvs = refs[2 * count :]
-    _, fs, pair, core, _ = place()
+def pair_kernel(count, pairs, fs_count, *refs):
+    partials, pieces = refs[:count], refs[count]
+    received, pieces_in = refs[count + 1 : 2 * count + 1], refs[2 * count + 1]
+    sends, recvs, z_sends, z_recvs = refs[2 * count + 2 :]
+    dp, fs, pair, core, _ = place()
     targets = [lax.rem(pair + o, pairs) for o in range(1, pairs)]
     peers = [(to * CORES + core, fs) for to in targets]
-    greet(peers)
+    z_targets = [lax.rem(fs + o, fs_count) for o in range(1, fs_count)]
+    greet(peers + [(dp, to) for to in z_targets])
     copies = [
         push(partial.at[to], landed.at[o], sends, recvs, (k, o), peer)
         for k, (partial, landed) in enumerate(zip(partials, received))
         for o, (to, peer) in enumerate(zip(targets, peers))
     ]
+    copies += [
+        push(pieces.at[to], pieces_in.at[o], z_sends, z_recvs, o, (dp, to))
+        for o, to in enumerate(z_targets)
+    ]
     for copy in copies:
         copy.wait()
 
 
-def exchange_call(kernel, partials, slots, collective_id, name):
+def twin_exchange(partials):
     count = len(partials)
     pairs = lax.axis_size("dp") // CORES
     return pl.pallas_call(
-        functools.partial(kernel, count, pairs),
-        out_shape=[jax.ShapeDtypeStruct((slots,) + p.shape[-2:], p.dtype) for p in partials],
+        functools.partial(twin_kernel, count, pairs),
+        out_shape=[jax.ShapeDtypeStruct((pairs,) + p.shape[-2:], p.dtype) for p in partials],
         in_specs=[pl.BlockSpec(memory_space=pl.ANY)] * count,
         out_specs=[pl.BlockSpec(memory_space=pl.ANY)] * count,
-        scratch_shapes=[pltpu.SemaphoreType.DMA((count, slots))] * 2,
-        compiler_params=pltpu.CompilerParams(collective_id=collective_id, has_side_effects=True),
-        name=name,
+        scratch_shapes=[pltpu.SemaphoreType.DMA((count, pairs))] * 2,
+        compiler_params=pltpu.CompilerParams(collective_id=1, has_side_effects=True),
+        name="twin_exchange",
     )(*partials)
 
 
-def reduce_all(partials):
+def pair_exchange(partials, pieces):
+    count = len(partials)
+    pairs, fs_count = lax.axis_size("dp") // CORES, lax.axis_size("fsdp")
+    slots = [(pairs - 1, p) for p in partials] + [(fs_count - 1, pieces)]
+    return pl.pallas_call(
+        functools.partial(pair_kernel, count, pairs, fs_count),
+        out_shape=[jax.ShapeDtypeStruct((n,) + p.shape[-2:], p.dtype) for n, p in slots],
+        in_specs=[pl.BlockSpec(memory_space=pl.ANY)] * len(slots),
+        out_specs=[pl.BlockSpec(memory_space=pl.ANY)] * len(slots),
+        scratch_shapes=[
+            pltpu.SemaphoreType.DMA((count, pairs - 1)),
+            pltpu.SemaphoreType.DMA((count, pairs - 1)),
+            pltpu.SemaphoreType.DMA((fs_count - 1,)),
+            pltpu.SemaphoreType.DMA((fs_count - 1,)),
+        ],
+        compiler_params=pltpu.CompilerParams(collective_id=2, has_side_effects=True),
+        name="pair_exchange",
+    )(*partials, pieces)
+
+
+def reduce_all(partials, pieces):
     dp_count = lax.axis_size("dp")
     pairs = dp_count // CORES
     dp = lax.axis_index("dp")
     core, pair = lax.rem(dp, CORES), dp // CORES
     split = [
-        p.astype(jnp.bfloat16).reshape(pairs, CORES, p.shape[0] // dp_count, p.shape[1])
+        p.reshape(pairs, CORES, p.shape[0] // dp_count, p.shape[1])
         for p in partials
     ]
-    landed = exchange_call(twin_kernel, split, pairs, 1, "twin_exchange")
+    landed = twin_exchange(split)
     chip = [
         (
             lax.dynamic_index_in_dim(p, core, axis=1, keepdims=False).astype(jnp.float32)
             + r.astype(jnp.float32)
-        ).astype(jnp.bfloat16)
+        ).astype(p.dtype)
         for p, r in zip(split, landed)
     ]
-    others = exchange_call(pair_kernel, chip, pairs - 1, 2, "pair_exchange")
-    return [
+    *others, pieces_in = pair_exchange(chip, pieces)
+    own_piece = lax.dynamic_index_in_dim(pieces, lax.axis_index("fsdp"), axis=0, keepdims=False)
+    tokens = own_piece.astype(jnp.float32) + jnp.sum(pieces_in.astype(jnp.float32), axis=0)
+    return tokens, [
         lax.dynamic_index_in_dim(p, pair, axis=0, keepdims=False).astype(jnp.float32)
         + jnp.sum(r.astype(jnp.float32), axis=0)
         for p, r in zip(chip, others)
@@ -353,9 +429,9 @@
     act2 = (cpart * conv).astype(jnp.bfloat16)
     hidden = inputs[0].astype(jnp.float32)
     normed1, scale1, _ = norm_forward(hidden, gain1)
-    resid = hidden + token_share(product(act2, out_rows))
+    resid = hidden + token_share(product(act2, out_rows), 3, "share_out")
     normed2, scale2, pre2 = norm_forward(resid, gain2)
-    act3_all = whole_sequence(pre2.astype(jnp.bfloat16))
+    act3_all = whole_sequence(pre2.astype(jnp.bfloat16), 4, "gather_ffn")
     gate_up = product(act3_all, gu_cols)
     gate, upval = gate_up[:, :hid], gate_up[:, hid:]
     sig = jax.nn.sigmoid(gate)
@@ -364,11 +440,11 @@
     dgate = (dact4 * upval * sig * (1.0 + gate * (1.0 - sig))).astype(jnp.bfloat16)
     dupval = (dact4 * gate * sig).astype(jnp.bfloat16)
     dgu = jnp.concatenate([dgate, dupval], axis=1)
-    dact3 = token_share(product_nt(dgu, gu_cols))
-    outputs = (resid + token_share(product(act4, down_rows))).astype(jnp.bfloat16)
+    dact3 = token_share(product_nt(dgu, gu_cols), 5, "share_ffn")
+    down_pieces = token_pieces(product(act4, down_rows))
     dnorm2, g_gain2 = norm_backward(dact3, normed2, scale2, gain2)
     dresid = grad_out.astype(jnp.float32) + dnorm2
-    dres_all = whole_sequence(dresid.astype(jnp.bfloat16))
+    dres_all = whole_sequence(dresid.astype(jnp.bfloat16), 6, "gather_dres")
     dact2 = product_nt(dres_all, out_rows)
     dcpart = dact2 * conv
     dconv = dact2 * cpart
@@ -379,30 +455,44 @@
     for offset in range(1, KW):
         dgated = dgated + taps32[offset] * leading(dconv, offset)
     dproj = jnp.concatenate([dgated * xpart, dcpart, dgated * bpart], axis=1).astype(jnp.bfloat16)
-    dact1 = token_share(product_nt(dproj, in_cols))
-    g_gu, g_down, g_in, g_out = reduce_all(
-        [
-            product_tn(act3_all, dgu),
-            product_tn(act4, grad_all),
-            product_tn(act1_all, dproj),
-            product_tn(act2, dres_all),
-        ]
-    )
+    dact1 = token_share_async(product_nt(dproj, in_cols))
     dnorm1, g_gain1 = norm_backward(dact1, normed1, scale1, gain1)
     grad_inputs = dresid + dnorm1
 
+    own_column = (jnp.arange(fs_count) == lax.axis_index("fsdp"))[None, None, :, None]
+    taps_spread = jnp.where(own_column, g_taps.reshape(KW, dp_count, 1, part), 0.0).reshape(KW, width)
+    small_grad = jnp.concatenate([g_gain1[None], g_gain2[None], taps_spread], axis=0)
+    small_grad = jnp.pad(small_grad, ((0, 8 - small_grad.shape[0]), (0, 0)))
+    small_grad = small_grad.reshape(8, dp_count, fs_count, part).transpose(1, 2, 0, 3)
+    small_grad = jnp.pad(small_grad, ((0, 0), (0, 0), (0, 0), (0, lanes - part)))
+    down_sum, (g_small, g_gu, g_down, g_in, g_out) = reduce_all(
+        [small_grad.reshape(dp_count * fs_count * 8, lanes)]
+        + [
+            grad.astype(jnp.bfloat16)
+            for grad in (
+                product_tn(act3_all, dgu),
+                product_tn(act4, grad_all),
+                product_tn(act1_all, dproj),
+                product_tn(act2, dres_all),
+            )
+        ],
+        down_pieces,
+    )
+    outputs = (resid + down_sum).astype(jnp.bfloat16)
     moved = jnp.concatenate([g_in, g_gu], axis=1).astype(jnp.bfloat16)
-    moved = exchange(moved.reshape(fs_count, part, 3 * quarter + 2 * hid)).astype(jnp.float32)
+    moved, small_parts = along_line(
+        [
+            moved.reshape(fs_count, part, 3 * quarter + 2 * hid),
+            g_small.reshape(fs_count, 8, lanes),
+        ],
+        False,
+        7,
+        "owner_exchange",
+    )
+    moved = moved.astype(jnp.float32)
     g_in_owned = moved[:, :, : 3 * quarter]
     g_gu_owned = moved[:, :, 3 * quarter :]
-    own_column = (jnp.arange(fs_count) == lax.axis_index("fsdp"))[None, None, :, None]
-    taps_spread = jnp.where(own_column, g_taps.reshape(KW, dp_count, 1, part), 0.0).reshape(KW, width)
-    small_owned = lax.psum_scatter(
-        jnp.concatenate([g_gain1[None], g_gain2[None], taps_spread], axis=0),
-        ("dp", "fsdp"),
-        scatter_dimension=1,
-        tiled=True,
-    )
+    small_owned = jnp.sum(small_parts, axis=0)[: KW + 2, :part]
     return (
         outputs[None],
         grad_inputs[None],

time: 526 us -> 381 us (0.72)
  waiting for transfers between devices: 227 us -> 8.16 us
  Pallas kernels: 129 us -> 255 us
  blocking collectives: 28.6 us -> 0 us
  between operations: 14.4 us -> 1.3 us
  starting transfers between devices: 20 us -> 7.17 us
    unnamed x4 -> x0, waiting for transfers between devices: 134 us -> none
    pallas_call x2 -> x7, Pallas kernels: 61.5 us -> 188 us  [the longest x5 123 us: along_line(): pl.pallas_call(functools.partial(line_kernel, count, fs_count, whole), ou...]
    all_gather x2 -> x0, waiting for transfers between devices: 52.9 us -> none  [whole_sequence(): return lax.all_gather(rows, 'fsdp', axis=0, tiled=True)]
    all_to_all x4 -> x1, waiting for transfers between devices: 39.8 us -> 8.16 us  [token_share_async(): lax.all_to_all(token_pieces(partial_value), 'fsdp', split_axis=0, concat_...]
    all_to_all x1 -> x0, blocking collectives: 28.6 us -> none  [token_share(): lax.all_to_all(pieces, 'fsdp', split_axis=0, concat_axis=0, tiled=True)]
    all_to_all x4 -> x1, starting transfers between devices: 19.5 us -> 7.17 us  [token_share_async(): lax.all_to_all(token_pieces(partial_value), 'fsdp', split_axis=0, concat_...]
    transpose x0 -> x3, local copies, waits for them, and re-layouts: none -> 5.63 us  [column_join(): blocks.reshape(fs_count, rows, lead, dp_count, inner)]
    reshape x6 -> x3, local copies, waits for them, and re-layouts: 9.44 us -> 3.86 us  [column_join(): blocks.reshape(fs_count, rows, lead, dp_count, inner)]
  transfers between devices with their start and end apart: 7 -> 1, of which waited for: 6 -> 1; matrix products, arithmetic and copies ran while one was open for 13% -> 4% of each run, Pallas kernels for 12% -> 0%
where the time goes in v3:
time: 381 us; the launch traced here: 379 us
  Pallas kernels  255 us (67%)
  other arithmetic  37.5 us (10%)
  local copies, waits for them, and re-layouts  35.3 us (9%)
  matrix products  34.6 us (9%)
  waiting for transfers between devices  8.16 us (2%)
  starting transfers between devices  7.17 us (2%)
    pallas_call x5, Pallas kernels, along_line(): pl.pallas_call(functools.partial(line_kernel, count, fs_count, whole), ou...  123 us
    pallas_call x1, Pallas kernels, gather_all(): pl.pallas_call(functools.partial(gather_kernel, pairs, fs_count), out_sha...  67.1 us
    pallas_call x1, Pallas kernels, pair_exchange(): pl.pallas_call(functools.partial(pair_kernel, count, pairs, fs_count), ou...  56.5 us
    dot_general x4, matrix products, product_tn(): lax.dot_general(left, right, (((0,), (0,)), ((), ())), preferred_element_...  12.9 us
    dot_general x4, matrix products, product_nt(): lax.dot_general(left, right, (((1,), (1,)), ((), ())), preferred_element_...  11.4 us
    dot_general x4, matrix products, product(): return jnp.dot(left, right, preferred_element_type=jnp.float32)  10.4 us
    reshape x3, local copies, waits for them, and re-layouts, column_join(): return pieces.reshape(rows, lead * dp_count * fs_count * inner)  9.73 us
    convert_element_type x4, other arithmetic, reduce_all(): chip = [(lax.dynamic_index_in_dim(p, core, axis=1, keepdims=False).astype...  8.8 us
  transfers between devices with their start and end apart: 1, of which 1 were waited for; matrix products, arithmetic and copies ran while one was open for 4% of the time, Pallas kernels for 0%

profile of v3, /device:TPU:0, one launch (start us, length us, event | category | flops | bytes accessed | tf_op | source)
XLA Modules:
  0.0 379.3 jit_solution(13409569086230814254)
XLA Ops:
  0.7 1.9 reshape.324
  7.8 67.1 %gather_all.1 = (bf16[4,128,1024]{2,1,0:T(8,128)(2,1)}, bf16[4,128,1024]{2,1,0:T(8,128)(2,1)}, bf16[8,4,8,128]{3,2,1,0:T(8,128)(2,1)}, bf16[8,4,32,768]{3,2,1,0:...) custom-call(bf16[128,1024]{1,0:T(8,128)(2,1)} %bitcast.174, ...), custom_call_target="tpu_custom_call" | custom-call | tf_op jit(solution)/shard_map/gather_all/pallas_call | solution.py:183
  84.7 25.4 %share_out.1 = bf16[4,128,1024]{2,1,0:T(8,128)(2,1)} custom-call(bf16[4,128,1024]{2,1,0:T(8,128)(2,1)} %bitcast.183), custom_call_target="tpu_custom_call" | custom-call | tf_op jit(solution)/shard_map/share_out/pallas_call | solution.py:225
  112.6 25.3 %gather_ffn.1 = bf16[4,128,1024]{2,1,0:T(8,128)(2,1)} custom-call(bf16[128,1024]{1,0:T(8,128)(2,1)} %multiply_convert_fusion.7.refs_0_), custom_call_target="tpu_custom_call" | custom-call | tf_op jit(solution)/shard_map/gather_ffn/pallas_call | solution.py:225
  138.0 5.4 %fusion.40 = f32[512,2304]{1,0:T(8,128)S(1)} fusion(bf16[512,1024]{1,0:T(8,128)(2,1)} %bitcast.200, bf16[1024,2304]{1,0:T(8,128)(2,1)} %bitcast.214), kind=kOutput, calls=%fused_computation.127 | convolution fusion | flops 2415919104 | bytes 10485760 | tf_op jit(solution)/shard_map/dot_general | solution.py:20
  143.4 3.5 multiply_convert_fusion.1
  146.9 3.8 %fusion.6 = bf16[512,1024]{1,0:T(8,128)(2,1)} fusion(bf16[1024,2304]{1,0:T(8,128)(2,1)S(1)} %bitcast.217, bf16[512,1152]{1,0:T(8,128)(2,1)S(1)} %get-tuple-element.69, bf16[512,1152]{1,0:T(8,128)(2,1)S(1)} %get-tuple-element.68), kind=kOutput, calls=%fused_computation.27 | convolution fusion | flops 2421161984 | bytes 8126464 | tf_op jit(solution)/shard_map/dot_general | solution.py:30
  150.7 25.6 %share_ffn.1 = bf16[4,128,1024]{2,1,0:T(8,128)(2,1)} custom-call(bf16[4,128,1024]{2,1,0:T(8,128)(2,1)} %bitcast.204), custom_call_target="tpu_custom_call" | custom-call | tf_op jit(solution)/shard_map/share_ffn/pallas_call | solution.py:225
  179.1 25.3 %gather_dres.1 = bf16[4,128,1024]{2,1,0:T(8,128)(2,1)} custom-call(bf16[128,1024]{1,0:T(8,128)(2,1)} %add_convert_fusion.refs_0_), custom_call_target="tpu_custom_call" | custom-call | tf_op jit(solution)/shard_map/gather_dres/pallas_call | solution.py:225
  204.4 2.1 multiply_reduce_fusion.3
  208.2 2.0 convolution_convert_fusion.3
  210.3 7.2 %all-to-all-start = ((bf16[4,128,1024]{2,1,0:T(8,128)(2,1)}), bf16[4,128,1024]{2,1,0:T(8,128)(2,1)}, u32[]{:S(2)}, u32[]{:S(2)}) async-start(bf16[4,128,1024]{2,1,0:T(8,128)(2,1)} %bitcast.203), calls=%async_computation | async-start | bytes 2097152 | tf_op jit(solution)/shard_map/all_to_all | solution.py:260
  217.4 2.2 convolution_convert_fusion.6
  220.5 3.4 convolution_convert_fusion.2
  224.0 2.9 convolution_convert_fusion.1
  226.9 2.5 convolution_convert_fusion.4
  229.4 4.4 %convolution_convert_fusion = bf16[1024,2304]{1,0:T(8,128)(2,1)} fusion(bf16[512,1024]{1,0:T(8,128)(2,1)S(1)} %bitcast.201, bf16[512,1152]{1,0:T(8,128)(2,1)S(1)} %copy-done.37, bf16[512,1152]{1,0:T(8,128)(2,1)S(1)} %copy-done.35), kind=kOutput, calls=%fused_computation | convolution fusion | flops 2422996992 | bytes 8126464 | tf_op jit(solution)/shard_map/dot_general | solution.py:24
  233.8 8.2 %all-to-all-done = bf16[4,128,1024]{2,1,0:T(8,128)(2,1)} async-done(((bf16[4,128,1024]{2,1,0:T(8,128)(2,1)}), bf16[4,128,1024]{2,1,0:T(8,128)(2,1)}, u32[]{:S(2)}, u32[]{:S(2)}) %all-to-all-start) | async-done | bytes 1048608 | tf_op jit(solution)/shard_map/all_to_all | solution.py:260
  244.6 8.5 %twin_exchange.1 = (f32[4,32,128]{2,1,0:T(8,128)}, bf16[4,128,2304]{2,1,0:T(8,128)(2,1)}, bf16[4,144,1024]{2,1,0:T(8,128)(2,1)}, bf16[4,128,768]{2,1,0:T(8,128)(2,1)}, bf16[4,32,1024]{2,1,0:T(8,128)(2,1)}) custom-call(f32[4,2,32,128]{3,2,1,0:T(8,128)} %bitcast.205, bf16[4,2,128,2304]{3,2,1,0:T(8,128)(2,1)} %bitcast.175, bf16[4,2,144,1024]{3,2,1,0:T(8,128)(2,1)} %bitcast.180, ...), custom_call_target="tpu_custom_call" | custom-call | tf_op jit(solution)/shard_map/twin_exchange/pallas_call | solution.py:305
  253.1 1.9 fusion.17.refs_4_
  256.6 3.1 fusion.1.refs_2_
  259.7 2.2 fusion.refs_1_
  263.4 56.5 %pair_exchange.1 = (f32[3,32,128]{2,1,0:T(8,128)}, bf16[3,128,2304]{2,1,0:T(8,128)(2,1)}, bf16[3,144,1024]{2,1,0:T(8,128)(2,1)}, bf16[3,128,768]{2,1,0:T(8,128)(...) custom-call(f32[4,32,128]{2,1,0:T(8,128)} %bitcast_add_fusion.1.refs_0_, ...), custom_call_target="tpu_custom_call" | custom-call | tf_op jit(solution)/shard_map/pair_exchange/pallas_call | solution.py:320
  323.3 1.9 convert_reduce_fusion
  326.3 21.4 %owner_exchange.1 = (bf16[4,32,3072]{2,1,0:T(8,128)(2,1)}, f32[4,8,128]{2,1,0:T(8,128)}) custom-call(bf16[4,32,3072]{2,1,0:T(8,128)(2,1)} %pad_maximum_fusion.6.refs_0_, f32[4,8,128]{2,1,0:T(8,128)} %bitcast_add_fusion.2.refs_1_), custom_call_target="tpu_custom_call" | custom-call | tf_op jit(solution)/shard_map/owner_exchange/pallas_call | solution.py:225
  351.3 2.0 fusion.38
  356.0 1.8 convert_add_fusion.6
  361.3 3.0 reshape.349
  366.7 3.0 reshape.347
  371.2 2.2 copy.38
  373.4 3.8 reshape.345
  377.1 2.2 fusion.15
  (161 shorter events, 46.2 us)
Async XLA Ops:
  0.6 2.4 copy-start.17
  5.1 2.2 copy-start.24
  5.1 2.2 copy-start.25
  84.7 26.9 %copy-start = (bf16[1,128,1024]{2,1,0:T(8,128)(2,1)S(1)}, bf16[1,128,1024]{2,1,0:T(8,128)(2,1)}, u32[]{:S(2)}) copy-start(bf16[1,128,1024]{2,1,0:T(8,128)(2,1)} %param.10) | copy-start | bytes 786436
  137.9 5.4 %copy-start.27 = (bf16[8,144,1024]{2,1,0:T(8,128)(2,1)S(1)}, bf16[8,144,1024]{2,1,0:T(8,128)(2,1)}, u32[]{:S(2)}) copy-start(bf16[8,144,1024]{2,1,0:T(8,128)(2,1)} %get-tuple-element.35) | copy-start | bytes 7077892
  137.9 5.4 %copy-start.31 = (bf16[4,128,1024]{2,1,0:T(8,128)(2,1)S(1)}, bf16[4,128,1024]{2,1,0:T(8,128)(2,1)}, u32[]{:S(2)}) copy-start(bf16[4,128,1024]{2,1,0:T(8,128)(2,1)} %get-tuple-element.36) | copy-start | bytes 3145732
  137.9 8.9 %slice-start = ((s8[4718592]{0:T(1024)(128)(4,1)}), s8[4194304]{0:T(1024)(128)(4,1)S(1)}, s32[]{:S(2)}) async-start(s8[4718592]{0:T(1024)(128)(4,1)} %bitcast.215), calls=%async_computation.1 | async-start | bytes 8388608
  143.4 3.5 slice-start.1
  146.9 3.8 %copy-start.34 = (bf16[512,1152]{1,0:T(8,128)(2,1)}, bf16[512,1152]{1,0:T(8,128)(2,1)S(1)}, u32[]{:S(2)}) copy-start(bf16[512,1152]{1,0:T(8,128)(2,1)S(1)} %get-tuple-element.68) | copy-start | bytes 3538948
  146.9 3.8 %copy-start.36 = (bf16[512,1152]{1,0:T(8,128)(2,1)}, bf16[512,1152]{1,0:T(8,128)(2,1)S(1)}, u32[]{:S(2)}) copy-start(bf16[512,1152]{1,0:T(8,128)(2,1)S(1)} %get-tuple-element.69) | copy-start | bytes 3538948
  206.8 3.4 copy-start.19
  206.9 3.4 copy-start.20
  210.2 7.2 %copy-start.2 = (bf16[4,128,1024]{2,1,0:T(8,128)(2,1)S(1)}, bf16[4,128,1024]{2,1,0:T(8,128)(2,1)}, u32[]{:S(2)}) copy-start(bf16[4,128,1024]{2,1,0:T(8,128)(2,1)} %gather_dres.1) | copy-start | bytes 3145732
  210.2 9.6 %copy-start.3 = (bf16[4,128,1024]{2,1,0:T(8,128)(2,1)S(1)}, bf16[4,128,1024]{2,1,0:T(8,128)(2,1)}, u32[]{:S(2)}) copy-start(bf16[4,128,1024]{2,1,0:T(8,128)(2,1)} %get-tuple-element.30) | copy-start | bytes 3145732
  210.3 31.7 %all-to-all-start = ((bf16[4,128,1024]{2,1,0:T(8,128)(2,1)}), bf16[4,128,1024]{2,1,0:T(8,128)(2,1)}, u32[]{:S(2)}, u32[]{:S(2)}) async-start(bf16[4,128,1024]{2,1,0:T(8,128)(2,1)} %bitcast.203), calls=%async_computation | async-start | bytes 2097152 | tf_op jit(solution)/shard_map/all_to_all | solution.py:260
  220.5 3.5 copy-start.32
  220.5 3.5 copy-start.33
  224.0 2.9 copy-start.28
  226.9 2.5 copy-start.13
  226.9 2.5 copy-start.35
  226.9 2.5 copy-start.37
  244.6 8.5 %copy-start.6 = (bf16[256,1024]{1,0:T(8,128)(2,1)S(1)}, bf16[256,1024]{1,0:T(8,128)(2,1)}, u32[]{:S(2)}) copy-start(bf16[256,1024]{1,0:T(8,128)(2,1)} %convolution_convert_fusion.6) | copy-start | bytes 1572868
  253.1 3.5 copy-start.4
  256.6 6.2 %copy-start.5 = (bf16[4,128,768]{2,1,0:T(8,128)(2,1)}, bf16[4,128,768]{2,1,0:T(8,128)(2,1)S(1)}, u32[]{:S(2)}) copy-start(bf16[4,128,768]{2,1,0:T(8,128)(2,1)S(1)} %fusion.4.refs_3_) | copy-start | bytes 2359300
  256.6 3.1 copy-start.7
  259.7 2.3 copy-start.15
  259.7 2.3 copy-start.23
  326.3 27.0 %copy-start.16 = (bf16[3,128,1024]{2,1,0:T(8,128)(2,1)S(1)}, bf16[3,128,1024]{2,1,0:T(8,128)(2,1)}, u32[]{:S(2)}) copy-start(bf16[3,128,1024]{2,1,0:T(8,128)(2,1)} %get-tuple-element.42) | copy-start | bytes 2359300
  349.6 4.7 %copy-start.21 = (bf16[3,32,1024]{2,1,0:T(8,128)(2,1)S(1)}, bf16[3,32,1024]{2,1,0:T(8,128)(2,1)}, u32[]{:S(2)}) copy-start(bf16[3,32,1024]{2,1,0:T(8,128)(2,1)} %get-tuple-element.48) | copy-start | bytes 589828
  351.3 4.5 %copy-start.14 = (bf16[3,144,1024]{2,1,0:T(8,128)(2,1)S(1)}, bf16[3,144,1024]{2,1,0:T(8,128)(2,1)}, u32[]{:S(2)}) copy-start(bf16[3,144,1024]{2,1,0:T(8,128)(2,1)} %get-tuple-element.49) | copy-start | bytes 2654212
  373.4 3.8 copy-start.9
  373.4 3.8 copy-start.12
  (9 other events, 13.8 us)

commit v4 on v3

--- a/solution.py
+++ b/solution.py
@@ -299,7 +299,7 @@
         copy.wait()
 
 
-def twin_exchange(partials):
+def twin_exchange(partials, collective_id, name):
     count = len(partials)
     pairs = lax.axis_size("dp") // CORES
     return pl.pallas_call(
@@ -308,12 +308,12 @@
         in_specs=[pl.BlockSpec(memory_space=pl.ANY)] * count,
         out_specs=[pl.BlockSpec(memory_space=pl.ANY)] * count,
         scratch_shapes=[pltpu.SemaphoreType.DMA((count, pairs))] * 2,
-        compiler_params=pltpu.CompilerParams(collective_id=1, has_side_effects=True),
-        name="twin_exchange",
+        compiler_params=pltpu.CompilerParams(collective_id=collective_id, has_side_effects=True),
+        name=name,
     )(*partials)
 
 
-def pair_exchange(partials, pieces):
+def pair_exchange(partials, pieces, collective_id, name):
     count = len(partials)
     pairs, fs_count = lax.axis_size("dp") // CORES, lax.axis_size("fsdp")
     slots = [(pairs - 1, p) for p in partials] + [(fs_count - 1, pieces)]
@@ -328,12 +328,12 @@
             pltpu.SemaphoreType.DMA((fs_count - 1,)),
             pltpu.SemaphoreType.DMA((fs_count - 1,)),
         ],
-        compiler_params=pltpu.CompilerParams(collective_id=2, has_side_effects=True),
-        name="pair_exchange",
+        compiler_params=pltpu.CompilerParams(collective_id=collective_id, has_side_effects=True),
+        name=name,
     )(*partials, pieces)
 
 
-def reduce_all(partials, pieces):
+def reduce_all(partials, pieces, ids, label):
     dp_count = lax.axis_size("dp")
     pairs = dp_count // CORES
     dp = lax.axis_index("dp")
@@ -342,7 +342,7 @@
         p.reshape(pairs, CORES, p.shape[0] // dp_count, p.shape[1])
         for p in partials
     ]
-    landed = twin_exchange(split)
+    landed = twin_exchange(split, ids[0], "twin_" + label)
     chip = [
         (
             lax.dynamic_index_in_dim(p, core, axis=1, keepdims=False).astype(jnp.float32)
@@ -350,7 +350,7 @@
         ).astype(p.dtype)
         for p, r in zip(split, landed)
     ]
-    *others, pieces_in = pair_exchange(chip, pieces)
+    *others, pieces_in = pair_exchange(chip, pieces, ids[1], "pair_" + label)
     own_piece = lax.dynamic_index_in_dim(pieces, lax.axis_index("fsdp"), axis=0, keepdims=False)
     tokens = own_piece.astype(jnp.float32) + jnp.sum(pieces_in.astype(jnp.float32), axis=0)
     return tokens, [
@@ -440,7 +440,15 @@
     dgate = (dact4 * upval * sig * (1.0 + gate * (1.0 - sig))).astype(jnp.bfloat16)
     dupval = (dact4 * gate * sig).astype(jnp.bfloat16)
     dgu = jnp.concatenate([dgate, dupval], axis=1)
-    dact3 = token_share(product_nt(dgu, gu_cols), 5, "share_ffn")
+    dact3, (g_gu, g_down) = reduce_all(
+        [
+            product_tn(act3_all, dgu).astype(jnp.bfloat16),
+            product_tn(act4, grad_all).astype(jnp.bfloat16),
+        ],
+        token_pieces(product_nt(dgu, gu_cols)),
+        (1, 2),
+        "ffn",
+    )
     down_pieces = token_pieces(product(act4, down_rows))
     dnorm2, g_gain2 = norm_backward(dact3, normed2, scale2, gain2)
     dresid = grad_out.astype(jnp.float32) + dnorm2
@@ -465,18 +473,18 @@
     small_grad = jnp.pad(small_grad, ((0, 8 - small_grad.shape[0]), (0, 0)))
     small_grad = small_grad.reshape(8, dp_count, fs_count, part).transpose(1, 2, 0, 3)
     small_grad = jnp.pad(small_grad, ((0, 0), (0, 0), (0, 0), (0, lanes - part)))
-    down_sum, (g_small, g_gu, g_down, g_in, g_out) = reduce_all(
+    down_sum, (g_small, g_in, g_out) = reduce_all(
         [small_grad.reshape(dp_count * fs_count * 8, lanes)]
         + [
             grad.astype(jnp.bfloat16)
             for grad in (
-                product_tn(act3_all, dgu),
-                product_tn(act4, grad_all),
                 product_tn(act1_all, dproj),
                 product_tn(act2, dres_all),
             )
         ],
         down_pieces,
+        (5, 8),
+        "mixer",
     )
     outputs = (resid + down_sum).astype(jnp.bfloat16)
     moved = jnp.concatenate([g_in, g_gu], axis=1).astype(jnp.bfloat16)

time: 381 us -> 381 us (level)
  Pallas kernels: 255 us -> 245 us
  other arithmetic: 37.5 us -> 41.9 us
    pallas_call x5 -> x4, Pallas kernels: 123 us -> 98.6 us  [along_line(): pl.pallas_call(functools.partial(line_kernel, count, fs_count, whole), ou...]
    pallas_call x1 -> x2, Pallas kernels: 56.5 us -> 69.3 us  [pair_exchange(): pl.pallas_call(functools.partial(pair_kernel, count, pairs, fs_count), ou...]
    pallas_call x1 -> x2, Pallas kernels: 8.51 us -> 10 us  [twin_exchange(): pl.pallas_call(functools.partial(twin_kernel, count, pairs), out_shape=[j...]
where the time goes in v4:
time: 381 us; the launch traced here: 380 us
  Pallas kernels  245 us (64%)
  other arithmetic  41.9 us (11%)
  local copies, waits for them, and re-layouts  38.3 us (10%)
  matrix products  35.9 us (9%)
  waiting for transfers between devices  9.68 us (3%)
  starting transfers between devices  7.77 us (2%)
    pallas_call x4, Pallas kernels, along_line(): pl.pallas_call(functools.partial(line_kernel, count, fs_count, whole), ou...  98.6 us
    pallas_call x2, Pallas kernels, pair_exchange(): pl.pallas_call(functools.partial(pair_kernel, count, pairs, fs_count), ou...  69.3 us
    pallas_call x1, Pallas kernels, gather_all(): pl.pallas_call(functools.partial(gather_kernel, pairs, fs_count), out_sha...  67.1 us
    dot_general x4, matrix products, product_tn(): lax.dot_general(left, right, (((0,), (0,)), ((), ())), preferred_element_...  14.3 us
    dot_general x4, matrix products, product_nt(): lax.dot_general(left, right, (((1,), (1,)), ((), ())), preferred_element_...  11.3 us
    dot_general x4, matrix products, product(): return jnp.dot(left, right, preferred_element_type=jnp.float32)  10.3 us
    convert_element_type x4, other arithmetic, reduce_all(): chip = [(lax.dynamic_index_in_dim(p, core, axis=1, keepdims=False).astype...  10.3 us
    pallas_call x2, Pallas kernels, twin_exchange(): pl.pallas_call(functools.partial(twin_kernel, count, pairs), out_shape=[j...  10 us
  transfers between devices with their start and end apart: 1, of which 1 were waited for; matrix products, arithmetic and copies ran while one was open for 4% of the time, Pallas kernels for 0%

profile of v4, /device:TPU:0, one launch (start us, length us, event | category | flops | bytes accessed | tf_op | source)
XLA Modules:
  0.0 379.7 jit_solution(2100228298317798540)
XLA Ops:
  0.7 1.9 reshape.305
  7.8 67.1 %gather_all.1 = (bf16[4,128,1024]{2,1,0:T(8,128)(2,1)}, bf16[4,128,1024]{2,1,0:T(8,128)(2,1)}, bf16[8,4,8,128]{3,2,1,0:T(8,128)(2,1)}, bf16[8,4,32,768]{3,2,1,0:...) custom-call(bf16[128,1024]{1,0:T(8,128)(2,1)} %bitcast.176, ...), custom_call_target="tpu_custom_call" | custom-call | tf_op jit(solution)/shard_map/gather_all/pallas_call | solution.py:183
  84.6 25.4 %share_out.1 = bf16[4,128,1024]{2,1,0:T(8,128)(2,1)} custom-call(bf16[4,128,1024]{2,1,0:T(8,128)(2,1)} %bitcast.185), custom_call_target="tpu_custom_call" | custom-call | tf_op jit(solution)/shard_map/share_out/pallas_call | solution.py:225
  112.5 25.3 %gather_ffn.1 = bf16[4,128,1024]{2,1,0:T(8,128)(2,1)} custom-call(bf16[128,1024]{1,0:T(8,128)(2,1)} %multiply_convert_fusion.7.refs_0_), custom_call_target="tpu_custom_call" | custom-call | tf_op jit(solution)/shard_map/gather_ffn/pallas_call | solution.py:225
  137.9 5.4 %fusion.42 = f32[512,2304]{1,0:T(8,128)S(1)} fusion(bf16[512,1024]{1,0:T(8,128)(2,1)} %bitcast.206, bf16[1024,2304]{1,0:T(8,128)(2,1)} %bitcast.219), kind=kOutput, calls=%fused_computation.130 | convolution fusion | flops 2415919104 | bytes 10485760 | tf_op jit(solution)/shard_map/dot_general | solution.py:20
  143.4 3.4 multiply_convert_fusion.1
  146.8 3.8 fusion.6
  150.6 4.3 %convolution_convert_fusion = bf16[1024,2304]{1,0:T(8,128)(2,1)} fusion(bf16[512,1024]{1,0:T(8,128)(2,1)S(1)} %bitcast.207, bf16[512,1152]{1,0:T(8,128)(2,1)S(1)} %get-tuple-element.71, bf16[512,1152]{1,0:T(8,128)(2,1)S(1)} %get-tuple-element.70), kind=kOutput, calls=%fused_computation | convolution fusion | flops 2422996992 | bytes 8126464 | tf_op jit(solution)/shard_map/dot_general | solution.py:24
  154.9 4.5 %convolution_convert_fusion.1 = bf16[1152,1024]{1,0:T(8,128)(2,1)} fusion(bf16[512,1152]{1,0:T(8,128)(2,1)} %get-tuple-element.72, bf16[512,1024]{1,0:T(8,128)(2,1)} %bitcast.227), kind=kOutput, calls=%fused_computation.3 | convolution fusion | flops 1209139200 | bytes 4587520 | tf_op jit(solution)/shard_map/dot_general | solution.py:24
  159.3 6.7 %twin_ffn.1 = (bf16[4,128,2304]{2,1,0:T(8,128)(2,1)}, bf16[4,144,1024]{2,1,0:T(8,128)(2,1)}) custom-call(bf16[4,2,128,2304]{3,2,1,0:T(8,128)(2,1)} %bitcast.177, bf16[4,2,144,1024]{3,2,1,0:T(8,128)(2,1)} %bitcast.182), custom_call_target="tpu_custom_call" | custom-call | tf_op jit(solution)/shard_map/twin_ffn/pallas_call | solution.py:305
  166.1 3.3 fusion.1.refs_1_
  169.3 3.7 fusion.refs_0_
  173.0 47.4 %pair_ffn.1 = (bf16[3,128,2304]{2,1,0:T(8,128)(2,1)}, bf16[3,144,1024]{2,1,0:T(8,128)(2,1)}, bf16[3,128,1024]{2,1,0:T(8,128)(2,1)}) custom-call(bf16[4,128,2304]{2,1,0:T(8,128)(2,1)} %fusion.refs_0_, bf16[4,144,1024]{2,1,0:T(8,128)(2,1)} %fusion.1.refs_1_, bf16[4,128,1024]{2,1,0:T(8,128)(2,1)} %bitcast.192), custom_call_target="tpu_custom_call" | custom-call | tf_op jit(solution)/shard_map/pair_ffn/pallas_call | solution.py:320
  223.1 1.9 add_convert_fusion.refs_0_
  225.0 21.8 %gather_dres.1 = bf16[4,128,1024]{2,1,0:T(8,128)(2,1)} custom-call(bf16[128,1024]{1,0:T(8,128)(2,1)} %add_convert_fusion.refs_0_), custom_call_target="tpu_custom_call" | custom-call | tf_op jit(solution)/shard_map/gather_dres/pallas_call | solution.py:225
  246.8 2.1 multiply_reduce_fusion.3
  250.6 2.0 convolution_convert_fusion.3
  252.6 7.8 %all-to-all-start = ((bf16[4,128,1024]{2,1,0:T(8,128)(2,1)}), bf16[4,128,1024]{2,1,0:T(8,128)(2,1)}, u32[]{:S(2)}, u32[]{:S(2)}) async-start(bf16[4,128,1024]{2,1,0:T(8,128)(2,1)} %bitcast.209), calls=%async_computation | async-start | bytes 2097152 | tf_op jit(solution)/shard_map/all_to_all | solution.py:260
  260.3 2.2 convolution_convert_fusion.6
  264.4 3.3 convolution_convert_fusion.2
  269.5 2.0 convert_reduce_fusion
  272.7 2.5 convolution_convert_fusion.4
  275.3 9.7 %all-to-all-done = bf16[4,128,1024]{2,1,0:T(8,128)(2,1)} async-done(((bf16[4,128,1024]{2,1,0:T(8,128)(2,1)}), bf16[4,128,1024]{2,1,0:T(8,128)(2,1)}, u32[]{:S(2)}, u32[]{:S(2)}) %all-to-all-start) | async-done | bytes 1048608 | tf_op jit(solution)/shard_map/all_to_all | solution.py:260
  287.7 3.3 twin_mixer.1
  295.8 21.9 %pair_mixer.1 = (f32[3,32,128]{2,1,0:T(8,128)}, bf16[3,128,768]{2,1,0:T(8,128)(2,1)}, bf16[3,32,1024]{2,1,0:T(8,128)(2,1)}, bf16[3,128,1024]{2,1,0:T(8,128)(2,1)}) custom-call(f32[4,32,128]{2,1,0:T(8,128)} %bitcast_add_fusion.1.refs_0_, bf16[4,128,768]{2,1,0:T(8,128)(2,1)} %copy-done.3, bf16[4,32,1024]{2,1,0:T(8,128)(2,1)} %fusion.22.refs_2_, ...), custom_call_target="tpu_custom_call" | custom-call | tf_op jit(solution)/shard_map/pair_mixer/pallas_call | solution.py:320
  323.0 26.0 %owner_exchange.1 = (bf16[4,32,3072]{2,1,0:T(8,128)(2,1)}, f32[4,8,128]{2,1,0:T(8,128)}) custom-call(bf16[4,32,3072]{2,1,0:T(8,128)(2,1)} %pad_maximum_fusion.6.refs_0_, f32[4,8,128]{2,1,0:T(8,128)} %bitcast_add_fusion.2.refs_1_), custom_call_target="tpu_custom_call" | custom-call | tf_op jit(solution)/shard_map/owner_exchange/pallas_call | solution.py:225
  352.6 2.1 fusion.40
  360.6 3.0 reshape.330
  367.0 3.0 reshape.328
  371.5 2.2 copy.38
  373.6 3.8 reshape.326
  377.4 2.3 fusion.15
  (148 shorter events, 53.4 us)
Async XLA Ops:
  0.6 2.4 copy-start.15
  2.5 2.0 copy-start.20
  5.1 2.2 copy-start.22
  5.1 2.2 copy-start.23
  5.1 2.2 copy-start.24
  78.7 1.7 copy-start.27
  81.5 1.7 copy-start.9
  84.6 26.9 %copy-start = (bf16[1,128,1024]{2,1,0:T(8,128)(2,1)S(1)}, bf16[1,128,1024]{2,1,0:T(8,128)(2,1)}, u32[]{:S(2)}) copy-start(bf16[1,128,1024]{2,1,0:T(8,128)(2,1)} %param.10) | copy-start | bytes 786436
  137.9 5.4 %copy-start.25 = (bf16[8,144,1024]{2,1,0:T(8,128)(2,1)S(1)}, bf16[8,144,1024]{2,1,0:T(8,128)(2,1)}, u32[]{:S(2)}) copy-start(bf16[8,144,1024]{2,1,0:T(8,128)(2,1)} %get-tuple-element.36) | copy-start | bytes 7077892
  137.9 5.4 %copy-start.29 = (bf16[4,128,1024]{2,1,0:T(8,128)(2,1)S(1)}, bf16[4,128,1024]{2,1,0:T(8,128)(2,1)}, u32[]{:S(2)}) copy-start(bf16[4,128,1024]{2,1,0:T(8,128)(2,1)} %get-tuple-element.37) | copy-start | bytes 3145732
  137.9 8.9 %slice-start = ((s8[4718592]{0:T(1024)(128)(4,1)}), s8[4194304]{0:T(1024)(128)(4,1)S(1)}, s32[]{:S(2)}) async-start(s8[4718592]{0:T(1024)(128)(4,1)} %bitcast.220), calls=%async_computation.1 | async-start | bytes 8388608
  143.4 3.4 slice-start.1
  146.8 3.8 copy-start.11
  166.1 3.3 copy-start.5
  220.4 2.6 copy-start.7
  249.0 1.6 copy-start.28
  249.1 3.4 copy-start.17
  249.2 3.3 copy-start.18
  252.6 7.8 %copy-start.1 = (bf16[4,128,1024]{2,1,0:T(8,128)(2,1)S(1)}, bf16[4,128,1024]{2,1,0:T(8,128)(2,1)}, u32[]{:S(2)}) copy-start(bf16[4,128,1024]{2,1,0:T(8,128)(2,1)} %gather_dres.1) | copy-start | bytes 3145732
  252.6 10.2 %copy-start.2 = (bf16[4,128,1024]{2,1,0:T(8,128)(2,1)S(1)}, bf16[4,128,1024]{2,1,0:T(8,128)(2,1)}, u32[]{:S(2)}) copy-start(bf16[4,128,1024]{2,1,0:T(8,128)(2,1)} %get-tuple-element.31) | copy-start | bytes 3145732
  252.6 32.5 %all-to-all-start = ((bf16[4,128,1024]{2,1,0:T(8,128)(2,1)}), bf16[4,128,1024]{2,1,0:T(8,128)(2,1)}, u32[]{:S(2)}, u32[]{:S(2)}) async-start(bf16[4,128,1024]{2,1,0:T(8,128)(2,1)} %bitcast.209), calls=%async_computation | async-start | bytes 2097152 | tf_op jit(solution)/shard_map/all_to_all | solution.py:260
  262.7 1.2 copy-start.12
  269.5 3.2 copy-start.26
  269.5 3.2 copy-start.30
  286.5 4.5 %copy-start.4 = (bf16[256,1024]{1,0:T(8,128)(2,1)S(1)}, bf16[256,1024]{1,0:T(8,128)(2,1)}, u32[]{:S(2)}) copy-start(bf16[256,1024]{1,0:T(8,128)(2,1)} %convolution_convert_fusion.6) | copy-start | bytes 1572868
  291.0 3.4 copy-start.13
  291.0 3.4 copy-start.21
  294.3 1.4 copy-start.3
  323.0 31.7 %copy-start.14 = (bf16[3,128,1024]{2,1,0:T(8,128)(2,1)S(1)}, bf16[3,128,1024]{2,1,0:T(8,128)(2,1)}, u32[]{:S(2)}) copy-start(bf16[3,128,1024]{2,1,0:T(8,128)(2,1)} %get-tuple-element.44) | copy-start | bytes 2359300
  350.8 4.8 %copy-start.19 = (bf16[3,32,1024]{2,1,0:T(8,128)(2,1)S(1)}, bf16[3,32,1024]{2,1,0:T(8,128)(2,1)}, u32[]{:S(2)}) copy-start(bf16[3,32,1024]{2,1,0:T(8,128)(2,1)} %get-tuple-element.50) | copy-start | bytes 589828
  373.6 3.8 copy-start.8
  373.6 3.8 copy-start.10
  (2 other events, 1.4 us)
